TPU v7x, 128 devices: a whole 4x4x4 slice. The times are simulated.
128 devices in a mesh: fer: 8 (over z, y_hi), bos: 16 (over y_lo, x, core).
Axes of the slice: x: 4, y: 4 (y_hi: 2, y_lo: 2; y = y_hi * 2 + y_lo), z: 4, core: 2. Of those that a mesh axis runs over, the one named last changes fastest.
Arguments:
- green: bfloat16 [4, 64, 9, 64, 128], P(None, 'fer', None, 'bos'), may hold values from -6 to 6
- bos_weight: bfloat16 [128, 9, 64, 128], P('bos'), may hold values from -12 to 12
- vertex: float32 [64, 128], P('fer', 'bos'), may hold values from 0.25 to 1.75
- block_order: int32 [16], replicated, may hold values from 0 to 15, each once
- window_start: int32 [1], replicated, may hold values from 0 to 64
Outputs:
- sigma: float32 [64, 64, 9, 128], P('bos', 'fer')
Inputs may be any that keep to these rules, and one draw needn't show every extreme that they name: block_order holds every block number once.
All inputs are finite; a program needn't handle non-finite values.
Results may differ from a plain program's by a relative error of at most 0.0003.
Values may be sent and summed in bfloat16 or wider, within the bound.
A program may use at most 128 MiB of HBM per device.

v0:
```python
import math

import jax
import jax.numpy as jnp
from jax import lax
from jax.sharding import PartitionSpec as P

HIGHEST = lax.Precision.HIGHEST


def passed_along(array, axis, by):
    size = lax.axis_size(axis)
    return lax.ppermute(array, axis, [(i, (i + by) % size) for i in range(size)])


def trig_tables(length):
    index = jnp.arange(length, dtype=jnp.int32)
    phase = (index[:, None] * index[None, :] % length).astype(jnp.float32) * (
        2.0 * math.pi / length
    )
    return (jnp.cos(phase), jnp.sin(phase))


def row_matrix(length, forward):
    cosine, sine = trig_tables(length)
    if forward:
        upper = jnp.concatenate([cosine, -sine], axis=1)
        lower = jnp.concatenate([sine, cosine], axis=1)
        block = jnp.concatenate([upper, lower], axis=0)
    else:
        upper = jnp.concatenate([cosine, sine], axis=1)
        lower = jnp.concatenate([-sine, cosine], axis=1)
        block = jnp.concatenate([upper, lower], axis=0) / length
    turned = jnp.concatenate([block[:, length:], -block[:, :length]], axis=1)
    return jnp.concatenate([block, turned], axis=1)


def col_tables(length, forward):
    cosine, sine = trig_tables(length)
    if forward:
        return (cosine, sine)
    return (cosine / length, -sine / length)


def row_step(field, matrix):
    return jnp.einsum("...c,cd->...d", field, matrix, precision=HIGHEST)


def col_step(halves, cos_part, sin_part):
    width = halves.shape[-1] // 2
    first = jnp.einsum("ax,nmxc->nmac", cos_part, halves[..., :width], precision=HIGHEST)
    return first + jnp.einsum("ax,nmxc->nmac", sin_part, halves[..., width:], precision=HIGHEST)


def body(green, bos_weight, vertex, block_order, window_start):
    num_fer = lax.axis_size("fer")
    fer_index = lax.axis_index("fer")
    bos_index = lax.axis_index("bos")
    num_slot = green.shape[0]
    window_dev = green.shape[1]
    orbitals = int(round(math.sqrt(green.shape[2])))
    bos_dev = bos_weight.shape[0]
    rows_all = bos_weight.shape[2]
    half_width = bos_weight.shape[3] // 2
    block_id = lax.dynamic_index_in_dim(block_order, bos_index, 0, keepdims=False)
    offset = window_start[0] + block_id * bos_dev
    shift_blocks = offset // window_dev
    inner = offset % window_dev
    shift_bits = shift_blocks % num_fer
    forward_rows = row_matrix(half_width, True)
    inverse_rows = row_matrix(half_width, False)
    forward_cos, forward_sin = col_tables(rows_all, True)
    inverse_cos, inverse_sin = col_tables(rows_all, False)
    full_rows = lax.all_gather(green, "bos", axis=3, tiled=True)
    current = full_rows
    for level in range(num_fer.bit_length() - 1):
        moved = passed_along(current, "fer", -(1 << level))
        current = jnp.where((shift_bits >> level) % 2 == 1, moved, current)
    sources = [current]
    for extra in range(2):
        current = passed_along(current, "fer", -1)
        sources.append(current)
    picked = []
    for extra in range(3):
        slot = (fer_index + shift_blocks + extra) // num_fer % num_slot
        picked.append(lax.dynamic_index_in_dim(sources[extra], slot, 0, keepdims=False))
    blocks = jnp.concatenate(picked, axis=0)
    halves = row_step(blocks.astype(jnp.float32), forward_rows)
    green_real = col_step(halves, forward_cos, forward_sin)
    weight_real = col_step(
        row_step(bos_weight.astype(jnp.float32), inverse_rows), inverse_cos, inverse_sin
    )
    total = jnp.zeros((window_dev, orbitals * orbitals, rows_all, 2 * half_width), jnp.float32)
    for column in range(bos_dev):
        part = lax.dynamic_slice_in_dim(green_real, inner + column, window_dev, 0)
        part = part.reshape(window_dev, orbitals, orbitals, 1, rows_all, 2 * half_width)
        factor = weight_real[column].reshape(1, 1, orbitals, orbitals, rows_all, 2 * half_width)
        green_re, green_im = (part[..., :half_width], part[..., half_width:])
        weight_re, weight_im = (factor[..., :half_width], factor[..., half_width:])
        real_part = jnp.sum(green_re * weight_re - green_im * weight_im, axis=2)
        imag_part = jnp.sum(green_re * weight_im + green_im * weight_re, axis=2)
        product = jnp.concatenate([real_part, imag_part], axis=-1)
        product = product.reshape(window_dev, orbitals * orbitals, rows_all, 2 * half_width)
        total = total + vertex[:, column][:, None, None, None] * product
    sigma_halves = row_step(-total, inverse_rows)
    width = sigma_halves.shape[-1] // 2
    first = jnp.einsum("ax,nmxc->anmc", inverse_cos, sigma_halves[..., :width], precision=HIGHEST)
    return lax.psum_scatter(
        first
        + jnp.einsum("ax,nmxc->anmc", inverse_sin, sigma_halves[..., width:], precision=HIGHEST),
        "bos",
        scatter_dimension=0,
        tiled=True,
    )


def solution(mesh):
    return jax.shard_map(
        body,
        mesh=mesh,
        in_specs=(
            P(None, "fer", None, "bos", None),
            P("bos", None, None, None),
            P("fer", "bos"),
            P(),
            P(),
        ),
        out_specs=P("bos", "fer", None, None),
        check_vma=False,
    )
```

profile of v0, /device:TPU:1, one launch (start us, length us, event | category | flops | bytes accessed | tf_op | source)
XLA Modules:
  0.0 764.2 jit_solution(11547539962003725166)
XLA Ops:
  8.4 42.7 %all-gather.2.cloned.1.call-done = bf16[4,8,9,64,128]{4,1,2,0,3:T(8,128)(2,1)} async-done(((bf16[4,8,9,4,128]{4,1,2,0,3:T(8,128)(2,1)}), bf16[4,8,9,64,128]{4,1,2,0,3:T(8,128)(2,1)}) %all-gather.2.cloned.1.call-update) | async-done | bytes 4718608 | tf_op jit(solution)/shard_map/all_gather | solution.py:74
  51.1 4.8 collective-permute-start
  58.5 98.6 %collective-permute-done = bf16[4,8,9,64,128]{4,1,2,0,3:T(8,128)(2,1)} collective-permute-done((bf16[4,8,9,64,128]{4,1,2,0,3:T(8,128)(2,1)}, bf16[4,8,9,64,128]{4,1,2,0,3:T(8,128)(2,1)}, u32[]{:S(2)}, u32[]{:S(2)}) %collective-permute-start) | collective-permute-done | bytes 4718624 | tf_op jit(solution)/shard_map/ppermute | solution.py:13
  157.1 5.0 broadcast_select_fusion
  163.7 100.9 %collective-permute-done.1 = bf16[4,8,9,64,128]{4,1,2,0,3:T(8,128)(2,1)} collective-permute-done((bf16[4,8,9,64,128]{4,1,2,0,3:T(8,128)(2,1)}, bf16[4,8,9,64,128]{4,1,2,0,3:T(8,128)(2,1)}, u32[]{:S(2)}, u32[]{:S(2)}) %collective-permute-start.1) | collective-permute-done | bytes 4718624 | tf_op jit(solution)/shard_map/ppermute | solution.py:13
  264.6 5.0 broadcast_select_fusion.1
  271.4 101.3 %collective-permute-done.2 = bf16[4,8,9,64,128]{4,1,2,0,3:T(8,128)(2,1)} collective-permute-done((bf16[4,8,9,64,128]{4,1,2,0,3:T(8,128)(2,1)}, bf16[4,8,9,64,128]{4,1,2,0,3:T(8,128)(2,1)}, u32[]{:S(2)}, u32[]{:S(2)}) %collective-permute-start.2) | collective-permute-done | bytes 4718624 | tf_op jit(solution)/shard_map/ppermute | solution.py:13
  372.7 2.8 broadcast_select_fusion.2
  377.8 7.0 collective-permute-start.3
  384.8 98.2 %collective-permute-done.3 = bf16[4,8,9,64,128]{4,1,2,0,3:T(8,128)(2,1)} collective-permute-done((bf16[4,8,9,64,128]{4,1,2,0,3:T(8,128)(2,1)S(1)}, bf16[4,8,9,64,128]{4,1,2,0,3:T(8,128)(2,1)}, u32[]{:S(2)}, u32[]{:S(2)}) %collective-permute-start.3) | collective-permute-done | bytes 4718624 | tf_op jit(solution)/shard_map/ppermute | solution.py:13
  483.0 6.4 collective-permute-start.4
  495.2 2.5 add_bitcast_fusion
  507.8 79.1 %collective-permute-done.4 = bf16[4,8,9,64,128]{4,1,2,0,3:T(8,128)(2,1)} collective-permute-done((bf16[4,8,9,64,128]{4,1,2,0,3:T(8,128)(2,1)}, bf16[4,8,9,64,128]{4,1,2,0,3:T(8,128)(2,1)}, u32[]{:S(2)}, u32[]{:S(2)}) %collective-permute-start.4) | collective-permute-done | bytes 4718624 | tf_op jit(solution)/shard_map/ppermute | solution.py:13
  588.6 6.1 fusion.4
  594.7 5.0 copy-done.2
  599.7 7.3 fusion
  607.0 9.5 %fusion.10 = f32[24,9,128,64]{2,3,1,0:T(8,128)S(1)} fusion(f32[24,9,128,64]{2,3,1,0:T(8,128)S(1)} %fusion, f32[24,9,64,256]{3,2,1,0:T(8,128)} %copy-done.2), kind=kOutput, calls=%fused_computation.29 | convolution fusion | flops 1360781312 | bytes 21233664 | tf_op jit(solution)/shard_map/ax,nmxc->nmac/dot_general | solution.py:51
  616.5 4.7 constant_dynamic-slice_fusion.7
  621.2 4.8 slice_bitcast_fusion.15
  628.5 3.1 slice_bitcast_fusion.11
  631.6 3.1 slice_bitcast_fusion.9
  640.5 3.7 subtract_reduce_fusion.7
  646.0 3.3 subtract_reduce_fusion.6
  651.7 3.3 subtract_reduce_fusion.5
  657.5 3.3 subtract_reduce_fusion.4
  662.6 3.5 subtract_reduce_fusion.3
  667.1 3.3 subtract_reduce_fusion.2
  671.4 3.3 subtract_reduce_fusion.1
  675.4 3.5 subtract_reduce_fusion
  679.7 4.8 fusion.21
  689.3 2.8 copy.16
  692.1 65.0 %reduce-scatter.2.cloned.1.call-done = f32[4,8,9,128]{3,1,2,0:T(8,128)} async-done(((f32[64,8,9,128]{3,1,2,0:T(8,128)}), f32[4,8,9,128]{3,1,2,0:T(8,128)}) %reduce-scatter.2.cloned.1.call-update) | async-done | bytes 147472 | tf_op jit(solution)/shard_map/reduce_scatter | solution.py:108
  (107 shorter events, 51.0 us)
Async XLA Ops:
  6.5 484.1 %copy-start = (bf16[8,9,64,128]{3,2,1,0:T(8,128)(2,1)S(1)}, bf16[8,9,64,128]{3,2,1,0:T(8,128)(2,1)}, u32[]{:S(2)}) copy-start(bf16[8,9,64,128]{3,2,1,0:T(8,128)(2,1)} %param.6) | copy-start | bytes 3538948
  6.5 44.6 %all-gather.2.cloned.1.call-start = ((), (), s32[]{:S(2)}) async-start(), calls=%async_computation.1 | async-start | bytes 5013504 | tf_op jit(solution)/shard_map/all_gather | solution.py:74
  8.4 748.7 %reduce-scatter.2.cloned.1.call-start = ((), (), s32[]{:S(2)}) async-start(), calls=%async_computation.2 | async-start | bytes 2506752 | tf_op jit(solution)/shard_map/reduce_scatter | solution.py:108
  51.1 106.0 %collective-permute-start = (bf16[4,8,9,64,128]{4,1,2,0,3:T(8,128)(2,1)}, bf16[4,8,9,64,128]{4,1,2,0,3:T(8,128)(2,1)}, u32[]{:S(2)}, u32[]{:S(2)}) collective-permute-start(bf16[4,8,9,64,128]{4,1,2,0,3:T(8,128)(2,1)} %all-gather.2.cloned.1.call-done), channel_id=1, source_target_pairs={{0,112},{16,0},{32,16},{48,32},{64,48},{80,64},{96,80},{112,96},{1... | collective-permute-start | bytes 14155784 | tf_op jit(solution)/shard_map/ppermute | solution.py:13
  162.1 102.5 %collective-permute-start.1 = (bf16[4,8,9,64,128]{4,1,2,0,3:T(8,128)(2,1)}, bf16[4,8,9,64,128]{4,1,2,0,3:T(8,128)(2,1)}, u32[]{:S(2)}, u32[]{:S(2)}) collective-permute-start(bf16[4,8,9,64,128]{4,1,2,0,3:T(8,128)(2,1)} %broadcast_select_fusion), channel_id=1, source_target_pairs={{0,96},{16,112},{32,0},{48,16},{64,32},{80,48},{96,64},{112,80},{1... | collective-permute-start | bytes 14155784 | tf_op jit(solution)/shard_map/ppermute | solution.py:13
  269.6 103.1 %collective-permute-start.2 = (bf16[4,8,9,64,128]{4,1,2,0,3:T(8,128)(2,1)}, bf16[4,8,9,64,128]{4,1,2,0,3:T(8,128)(2,1)}, u32[]{:S(2)}, u32[]{:S(2)}) collective-permute-start(bf16[4,8,9,64,128]{4,1,2,0,3:T(8,128)(2,1)} %broadcast_select_fusion.1), channel_id=1, source_target_pairs={{0,64},{16,80},{32,96},{48,112},{64,0},{80,16},{96,32},{112,48},{1... | collective-permute-start | bytes 14155784 | tf_op jit(solution)/shard_map/ppermute | solution.py:13
  271.4 217.9 %copy-start.29 = (f32[8,8]{1,0:T(8,128)S(1)}, f32[8,8]{1,0:T(8,128)}, u32[]{:S(2)}) copy-start(f32[8,8]{1,0:T(8,128)} %param.7) | copy-start | bytes 772
  375.6 2.2 copy-start.13
  377.8 105.2 %collective-permute-start.3 = (bf16[4,8,9,64,128]{4,1,2,0,3:T(8,128)(2,1)S(1)}, bf16[4,8,9,64,128]{4,1,2,0,3:T(8,128)(2,1)}, u32[]{:S(2)}, u32[]{:S(2)}) collective-permute-start(bf16[4,8,9,64,128]{4,1,2,0,3:T(8,128)(2,1)S(1)} %broadcast_select_fusion.2), channel_id=1, source_target_pairs={{0,112},{16,0},{32,16},{48,32},{64,48},{80,64},{96,80},{112,96},{1... | collective-permute-start | bytes 14155784 | tf_op jit(solution)/shard_map/ppermute | solution.py:13
  483.0 103.9 %collective-permute-start.4 = (bf16[4,8,9,64,128]{4,1,2,0,3:T(8,128)(2,1)}, bf16[4,8,9,64,128]{4,1,2,0,3:T(8,128)(2,1)}, u32[]{:S(2)}, u32[]{:S(2)}) collective-permute-start(bf16[4,8,9,64,128]{4,1,2,0,3:T(8,128)(2,1)} %collective-permute-done.3), channel_id=1, source_target_pairs={{0,112},{16,0},{32,16},{48,32},{64,48},{80,64},{96,80},{112,96},{1... | collective-permute-start | bytes 14155784 | tf_op jit(solution)/shard_map/ppermute | solution.py:13
  490.7 2.1 copy-start.27
  594.6 5.1 copy-start.2
  621.2 4.8 copy-start.5
  626.0 2.5 copy-start.4
  628.5 3.2 copy-start.3
  638.7 1.7 copy-start.12
  638.8 1.7 copy-start.25
  638.8 1.7 copy-start.26
  644.2 1.7 copy-start.11
  644.2 1.7 copy-start.23
  644.2 1.7 copy-start.24
  649.3 1.7 copy-start.9
  649.3 2.4 copy-start.10
  649.3 2.4 copy-start.21
  649.3 2.4 copy-start.22
  655.0 1.7 copy-start.7
  655.0 2.4 copy-start.8
  655.1 2.4 copy-start.19
  655.1 2.4 copy-start.20
  660.8 1.7 copy-start.6
  660.8 1.7 copy-start.18
  689.2 67.8 %copy-start.1 = (bf16[8,9,64,128]{3,2,1,0:T(8,128)(2,1)S(1)}, bf16[8,9,64,128]{3,2,1,0:T(8,128)(2,1)}, u32[]{:S(2)}) copy-start(bf16[8,9,64,128]{3,2,1,0:T(8,128)(2,1)} %param.6) | copy-start | bytes 3538948
  (6 other events, 6.3 us)
Sparse Core Ops, SparseCore 0:
  9.1 41.9 all-gather.1
  692.2 64.8 reduce-scatter.1
where the time goes:
time: 771 us; the launch traced here: 764 us
  waiting for transfers between devices  586 us (76%)
  local copies, waits for them, and re-layouts  55.9 us (7%)
  other arithmetic  45.9 us (6%)
  matrix products  39.4 us (5%)
  starting transfers between devices  21.6 us (3%)
  between operations  15.5 us (2%)
    ppermute x5, waiting for transfers between devices, passed_along(): lax.ppermute(array, axis, [(i, (i + by) % size) for i in range(size)])  478 us
    reduce_scatter x1, waiting for transfers between devices, body(): lax.psum_scatter(first + jnp.einsum('ax,nmxc->anmc', inverse_sin, sigma_h...  65 us
    all_gather x1, waiting for transfers between devices, body(): full_rows = lax.all_gather(green, 'bos', axis=3, tiled=True)  42.7 us
    reduce_sum x8, other arithmetic, body(): real_part = jnp.sum(green_re * weight_re - green_im * weight_im, axis=2)  27.1 us
    mul x16, local copies, waits for them, and re-layouts, body(): real_part = jnp.sum(green_re * weight_re - green_im * weight_im, axis=2)  24.8 us
    ppermute x5, starting transfers between devices, passed_along(): lax.ppermute(array, axis, [(i, (i + by) % size) for i in range(size)])  21.5 us
    unnamed x63, local copies, waits for them, and re-layouts  16.4 us
  transfers between devices with their start and end apart: 7, of which 7 were waited for; matrix products, arithmetic and copies ran while one was open for 3% of the time, Pallas kernels for 0%

commit v1 on v0

v1 whole, which is shorter than its diff:
```python
import functools
import math

import jax
import jax.numpy as jnp
import ml_dtypes
import numpy as np
from jax import lax
from jax.experimental import pallas as pl
from jax.experimental.pallas import tpu as pltpu
from jax.sharding import PartitionSpec as P

MESH = pl.DeviceIdType.MESH
BF16 = jnp.bfloat16
F32 = jnp.float32
L = 64
FER = 8
BOS = 16
VMEM_LIMIT = 56 * 1024 * 1024


def split_np(m):
    hi = m.astype(ml_dtypes.bfloat16)
    lo = (m - hi.astype(np.float64)).astype(ml_dtypes.bfloat16)
    return np.stack([hi, lo])


def trig(a, b):
    t = 2.0 * math.pi * ((np.asarray(a)[:, None] * np.asarray(b)[None, :]) % L) / L
    return np.cos(t), np.sin(t)


def complex_map(c, s, sign):
    m = np.zeros((2, 2) + c.shape)
    m[0, 0], m[1, 1] = c, c
    m[1, 0], m[0, 1] = -sign * s, sign * s
    return m


def first_matrix(sign, scale):
    c, s = trig(np.arange(L), np.arange(L))
    m = complex_map(c, s, sign) * scale
    return split_np(m.transpose(1, 3, 0, 2).reshape(2 * L, 2 * L))


def second_matrix(sign, scale, grouped):
    c, s = trig(np.arange(L), np.arange(L))
    m = complex_map(c, s, sign) * scale
    m = m.reshape(2, 2, L, 2, 2, 16)
    full = np.zeros((2, 2, L, 2, 2, 2, 2, 16))
    for pair in range(2):
        full[:, pair, :, :, :, pair] = m.transpose(0, 2, 3, 4, 1, 5)
    if not grouped:
        full = full.transpose(0, 1, 2, 3, 5, 6, 4, 7)
    return split_np(full.reshape(4 * L, 4 * L))


def out_x_matrix():
    c, s = trig(np.arange(L), np.arange(L))
    m = complex_map(c, s, 1.0) * (-1.0 / L)
    m = m.reshape(2, 2, 2, 2, 16, 16, 4)
    full = np.zeros((3, 16, 2, 4, 2, 2, 4, 2, 16))
    for b in range(3):
        full[b, :, :, :, :, :, b] = m.transpose(5, 1, 6, 2, 3, 0, 4)
    return split_np(full.reshape(3, 128, 512))


def out_y_matrix():
    c, s = trig(np.arange(L), np.arange(L))
    m = complex_map(c, s, 1.0) / L
    m = m.reshape(2, 2, 16, 4, L)
    full = np.zeros((4, 16, 2, 4, 4, 2, L))
    for k in range(4):
        full[:, :, :, k, k] = m.transpose(3, 2, 0, 1, 4)
    return split_np(full.reshape(512, 512))


def mm(a, b):
    return jnp.dot(a, b, preferred_element_type=F32)


def nt(a, b):
    return lax.dot_general(a, b, (((1,), (1,)), ((), ())), preferred_element_type=F32)


def halves(x):
    hi = x.astype(BF16)
    return hi, (x - hi.astype(F32)).astype(BF16)


def exchange_green(green, vertex):
    def kernel(g_ref, v_ref, x_ref, vo_ref, gs, gr, vs, vr, own):
        me = lax.axis_index("bos")
        mine = [
            pltpu.make_async_copy(g_ref.at[:, me // 8, me % 8], x_ref.at[:, :, me], own.at[0]),
            pltpu.make_async_copy(v_ref, vo_ref.at[me], own.at[1]),
        ]
        copies = []
        for i in range(1, BOS):
            to = lax.rem(me + i, BOS)
            for k, (src, dst, ss, rs) in enumerate(
                (
                    (g_ref.at[:, to // 8, lax.rem(to, 8)], x_ref.at[:, :, me], gs, gr),
                    (v_ref, vo_ref.at[me], vs, vr),
                )
            ):
                copies.append(
                    pltpu.make_async_remote_copy(
                        src_ref=src,
                        dst_ref=dst,
                        send_sem=ss.at[i],
                        recv_sem=rs.at[i],
                        device_id={"bos": to},
                        device_id_type=MESH,
                    )
                )
        for c in copies:
            c.start()
        for c in mine:
            c.start()
        for c in mine:
            c.wait()
        for c in copies:
            c.wait()

    any_ = pl.BlockSpec(memory_space=pltpu.VMEM)
    return pl.pallas_call(
        kernel,
        out_shape=(
            jax.ShapeDtypeStruct((2, 9, BOS, 4, 128), BF16),
            jax.ShapeDtypeStruct((BOS, 8, 8), F32),
        ),
        in_specs=[any_, any_],
        out_specs=(any_, any_),
        scratch_shapes=[pltpu.SemaphoreType.DMA((BOS,))] * 4 + [pltpu.SemaphoreType.DMA((2,))],
        compiler_params=pltpu.CompilerParams(has_side_effects=True),
        name="exchange_green",
    )(green, vertex)


def exchange_positions(sent):
    count = FER * BOS

    def kernel(s_ref, r_ref, ss, rs, own):
        f, j = lax.axis_index("fer"), lax.axis_index("bos")
        me = j * FER + f
        row = count - 1 - ((j // 8) * 64 + f * 8 + lax.rem(j, 8))
        mine = pltpu.make_async_copy(s_ref.at[me], r_ref.at[row], own)
        mine.start()

        def send(i, carry):
            to = lax.rem(me + i, count)
            pltpu.make_async_remote_copy(
                src_ref=s_ref.at[to],
                dst_ref=r_ref.at[row],
                send_sem=ss,
                recv_sem=rs,
                device_id={"fer": lax.rem(to, FER), "bos": to // FER},
                device_id_type=MESH,
            ).start()
            return carry

        lax.fori_loop(1, count, send, 0)
        mine.wait()
        whole = pltpu.make_async_remote_copy(
            src_ref=s_ref.at[pl.ds(0, count - 1)],
            dst_ref=r_ref.at[pl.ds(0, count - 1)],
            send_sem=ss,
            recv_sem=rs,
            device_id={"fer": f, "bos": lax.rem(j + 1, BOS)},
            device_id_type=MESH,
        )
        whole.wait()

    any_ = pl.BlockSpec(memory_space=pltpu.VMEM)
    return pl.pallas_call(
        kernel,
        out_shape=jax.ShapeDtypeStruct((count, 16, 128), F32),
        in_specs=[any_],
        out_specs=any_,
        scratch_shapes=[pltpu.SemaphoreType.DMA] * 3,
        compiler_params=pltpu.CompilerParams(has_side_effects=True, vmem_limit_bytes=VMEM_LIMIT),
        name="exchange_positions",
    )(sent)


def exchange_axis(sent, axis, size, pick, out_shape, name):
    def kernel(s_ref, r_ref, ss, rs, own):
        me = lax.axis_index(axis)
        mine = pltpu.make_async_copy(pick(s_ref, me), r_ref.at[me], own)
        copies = []
        for i in range(1, size):
            to = lax.rem(me + i, size)
            copies.append(
                pltpu.make_async_remote_copy(
                    src_ref=pick(s_ref, to),
                    dst_ref=r_ref.at[me],
                    send_sem=ss.at[i],
                    recv_sem=rs.at[i],
                    device_id={axis: to},
                    device_id_type=MESH,
                )
            )
        for c in copies:
            c.start()
        mine.start()
        mine.wait()
        for c in copies:
            c.wait()

    any_ = pl.BlockSpec(memory_space=pltpu.VMEM)
    return pl.pallas_call(
        kernel,
        out_shape=jax.ShapeDtypeStruct(out_shape, F32),
        in_specs=[any_],
        out_specs=any_,
        scratch_shapes=[pltpu.SemaphoreType.DMA((size,))] * 2 + [pltpu.SemaphoreType.DMA],
        compiler_params=pltpu.CompilerParams(has_side_effects=True),
        name=name,
    )(sent)


def to_positions(planes, weight, vertex_row, mats):
    def kernel(x_ref, w_ref, v_ref, g1, g2, w1, w2, s_ref):
        def both(x, m1, m2, row):
            z = nt(m1[0], x) + nt(m1[1], x)
            hi, lo = halves(jnp.concatenate([z[:L], z[L:]], axis=1))
            y = mm(hi, m2[0]) + mm(hi, m2[1]) + mm(lo, m2[0])
            for half in range(2):
                s_ref[:, half, row, :] = y[:, half * 128 : half * 128 + 128]

        for ac in range(9):
            both(jnp.concatenate([x_ref[0, ac], x_ref[1, ac]], axis=0), g1, g2, ac)
        for k in range(5):
            x = w_ref[0, 128 * k : 128 * k + 128] if k < 4 else w_ref[0, 512:576]
            if k == 4:
                x = jnp.concatenate([x, jnp.zeros((64, 128), BF16)], axis=0)
            both(x, w1, w2, 9 + k)
        s_ref[:, :, 14, :] = jnp.broadcast_to(v_ref[...].reshape(1, 1, 128), (L, 2, 128))
        s_ref[:, :, 15, :] = jnp.zeros((L, 2, 128), F32)

    vm = pl.BlockSpec(memory_space=pltpu.VMEM)
    return pl.pallas_call(
        kernel,
        out_shape=jax.ShapeDtypeStruct((L, 2, 16, 128), F32),
        in_specs=[vm] * 7,
        out_specs=vm,
        compiler_params=pltpu.CompilerParams(vmem_limit_bytes=VMEM_LIMIT),
        name="to_positions",
    )(planes, weight, vertex_row, *mats)


def contract(received, block_order, window_start):
    def kernel(bo, ws, r_ref, o_ref, gt, wk, wb, vert, hh, hl):
        s = ws[0]
        lane = lax.broadcasted_iota(jnp.int32, (128, 128), 1)
        for ac in range(9):
            gt[ac] = pltpu.roll(r_ref[:, ac, :].T, s, axis=1)
        for j in range(BOS):
            base = (1 - j // 8) * 64 + (7 - j % 8)
            to = pl.multiple_of(8 * (15 - bo[j]), 8)
            for k in range(5):
                wk[k, pl.ds(to, 8), :] = r_ref[pl.ds(base, 8, stride=8), 9 + k, :]
        for rg in range(2):
            for c in range(3):
                t = jnp.zeros((128, 128), F32)
                for b in range(3):
                    k, odd = divmod(3 * c + b, 2)
                    by = (32 * b - 64 * rg - 32 * odd) % 128
                    piece = wk[k]
                    if by:
                        piece = pltpu.roll(piece, by, axis=1)
                    t = jnp.where(lane // 32 == b, piece, t)
                turned = jnp.where(
                    lane % 32 < 16, -pltpu.roll(t, 112, axis=1), pltpu.roll(t, 16, axis=1)
                )
                for ri, part in enumerate((t, turned)):
                    hi, lo = halves(part)
                    rows = slice((2 * c + ri) * 128, (2 * c + ri) * 128 + 128)
                    wb[rg, rows, 0:128] = hi
                    wb[rg, rows, 128:256] = lo
        lane8 = lax.broadcasted_iota(jnp.int32, (8, 128), 1)
        raw = [r_ref[8 * (7 - o) : 8 * (7 - o) + 8, 14, :] for o in range(8)]
        turned = [jnp.zeros((8, 128), F32) for _ in range(8)]
        for j in range(BOS):
            by = lax.rem(8 * (j - bo[j]) + 128, 128)
            here = lane8 // 8 == 15 - bo[j]
            for o in range(8):
                turned[o] = jnp.where(here, pltpu.roll(raw[o], by, axis=1), turned[o])
        for o in range(8):
            vert[8 * o : 8 * o + 8, :] = turned[o]
        o_ref[...] = jnp.zeros_like(o_ref)

        row8 = lax.broadcasted_iota(jnp.int32, (8, 128), 0)
        back = s + row8
        origin = (lane8 - back + 256) % 128
        upper = [origin >= 128 - back - 8 * o for o in range(8)]

        def skewed(ac, row):
            y = jnp.broadcast_to(gt[ac, pl.ds(row, 1), :], (8, 128))
            for bit in (1, 2, 4):
                y = jnp.where(row8 & bit != 0, pltpu.roll(y, bit, axis=1), y)
            return y

        for rg in range(2):

            def step(r16, carry):
                r = rg * 16 + r16
                for a in range(3):
                    for c in range(3):
                        for ri in range(2):
                            first = skewed(3 * a + c, 64 + ri * 32 + r)
                            second = skewed(3 * a + c, ri * 32 + r)
                            octets = []
                            for o in range(8):
                                y = jnp.where(upper[o], first, second)
                                octets.append(pltpu.roll(y, 8 * o, axis=1) if o else y)
                            h = jnp.concatenate(octets, axis=0)
                            hi, lo = halves(h * vert[...])
                            at = (slice(64 * a, 64 * a + 64), slice((2 * c + ri) * 128, (2 * c + ri) * 128 + 128))
                            hh[at] = hi
                            hl[at] = lo
                acc = mm(hh[...], wb[rg]) + mm(hl[...], wb[rg])
                res = (acc[:, :128] + acc[:, 128:]).reshape(3, 64, 128)
                here = lax.broadcasted_iota(jnp.int32, (3, 64, 128), 2) % 16 == r16
                o_ref[rg] = jnp.where(here, res, o_ref[rg])
                return carry

            lax.fori_loop(0, 16, step, 0)

    vm = pl.BlockSpec(memory_space=pltpu.VMEM)
    sm = pl.BlockSpec(memory_space=pltpu.SMEM)
    return pl.pallas_call(
        kernel,
        out_shape=jax.ShapeDtypeStruct((2, 3, 64, 128), F32),
        in_specs=[sm, sm, vm],
        out_specs=vm,
        scratch_shapes=[
            pltpu.VMEM((9, 128, 128), F32),
            pltpu.VMEM((5, 128, 128), F32),
            pltpu.VMEM((2, 768, 256), BF16),
            pltpu.VMEM((64, 128), F32),
            pltpu.VMEM((192, 768), BF16),
            pltpu.VMEM((192, 768), BF16),
        ],
        compiler_params=pltpu.CompilerParams(vmem_limit_bytes=VMEM_LIMIT),
        name="contract",
    )(block_order, window_start, received)


def back_x(got, mat):
    def kernel(b_ref, m_ref, f_ref, lh, ll):
        lh[96:, :] = jnp.zeros((32, 512), BF16)
        ll[96:, :] = jnp.zeros((32, 512), BF16)
        for ryl in range(4):
            for half in range(2):
                for rg in range(2):
                    x = b_ref[2 * ryl + half, rg].reshape(24, 128)
                    hi, lo = halves(x)
                    at = (slice(24 * ryl, 24 * ryl + 24), slice((2 * half + rg) * 128, (2 * half + rg) * 128 + 128))
                    lh[at] = hi
                    ll[at] = lo
        for b in range(3):
            y = nt(m_ref[0, b], lh[...]) + nt(m_ref[0, b], ll[...]) + nt(m_ref[1, b], lh[...])
            f_ref[:, :, b * 128 : b * 128 + 128] = y.reshape(16, 8, 128)

    vm = pl.BlockSpec(memory_space=pltpu.VMEM)
    return pl.pallas_call(
        kernel,
        out_shape=jax.ShapeDtypeStruct((BOS, 8, 384), F32),
        in_specs=[vm, vm],
        out_specs=vm,
        scratch_shapes=[pltpu.VMEM((128, 512), BF16)] * 2,
        name="back_x",
    )(got, mat)


def back_y(got, mat):
    def kernel(e_ref, m_ref, o_ref, lh, ll):
        for b in range(3):
            t = e_ref[:, :, b * 128 : b * 128 + 128].reshape(128, 128).T
            hi, lo = halves(t)
            for ryl in range(4):
                at = (slice(24 * b, 24 * b + 24), slice(128 * ryl, 128 * ryl + 128))
                lh[at] = hi[24 * ryl : 24 * ryl + 24]
                ll[at] = lo[24 * ryl : 24 * ryl + 24]
        y = mm(lh[...], m_ref[0]) + mm(ll[...], m_ref[0]) + mm(lh[...], m_ref[1])
        for b in range(3):
            for a in range(3):
                for k in range(4):
                    o_ref[k, 3 * a + b] = y[24 * b + 8 * a : 24 * b + 8 * a + 8, 128 * k : 128 * k + 128]

    vm = pl.BlockSpec(memory_space=pltpu.VMEM)
    return pl.pallas_call(
        kernel,
        out_shape=jax.ShapeDtypeStruct((4, 9, 8, 128), F32),
        in_specs=[vm, vm],
        out_specs=vm,
        scratch_shapes=[pltpu.VMEM((72, 512), BF16)] * 2,
        name="back_y",
    )(got, mat)


def body(green, bos_weight, vertex, block_order, window_start):
    f, j = lax.axis_index("fer"), lax.axis_index("bos")
    planes, rows = exchange_green(green.reshape(2, 2, 8, 9, 4, 128), vertex)
    rows = rows.transpose(1, 0, 2).reshape(8, 128)[:, ::-1]
    row = lax.dynamic_slice_in_dim(rows, 7 - j % 8, 1, 0)
    weight = lax.dynamic_slice_in_dim(bos_weight, f, 1, 0).reshape(1, 576, 128)
    mats = [
        jnp.asarray(first_matrix(-1.0, 1.0)),
        jnp.asarray(second_matrix(-1.0, 1.0, False)),
        jnp.asarray(first_matrix(1.0, 1.0 / L)),
        jnp.asarray(second_matrix(1.0, 1.0 / L, True)),
    ]
    sent = to_positions(planes.reshape(2, 9, L, 128), weight, row, mats)
    got = exchange_positions(sent.reshape(128, 16, 128))
    part = contract(got, block_order, window_start)
    octets = exchange_axis(
        part, "fer", FER, lambda ref, to: ref.at[:, :, pl.ds(pl.multiple_of(8 * to, 8), 8), :], (FER, 2, 3, 8, 128), "exchange_octets"
    )
    quads = back_x(octets, jnp.asarray(out_x_matrix()))
    last = exchange_axis(quads, "bos", BOS, lambda ref, to: ref.at[to], (BOS, 8, 384), "exchange_rows")
    return back_y(last, jnp.asarray(out_y_matrix())).transpose(0, 2, 1, 3)


def solution(mesh):
    return jax.shard_map(
        body,
        mesh=mesh,
        in_specs=(
            P(None, "fer", None, "bos", None),
            P("bos", None, None, None),
            P("fer", "bos"),
            P(),
            P(),
        ),
        out_specs=P("bos", "fer", None, None),
        check_vma=False,
    )
```

time: 771 us -> 114 us (0.15)
  waiting for transfers between devices: 586 us -> 0 us
  Pallas kernels: 0 us -> 111 us
  local copies, waits for them, and re-layouts: 55.9 us -> 2.24 us
  other arithmetic: 45.9 us -> 0 us
  matrix products: 39.4 us -> 0 us
  starting transfers between devices: 21.6 us -> 0 us
  between operations: 15.5 us -> 0.69 us
    ppermute x5 -> x0, waiting for transfers between devices: 478 us -> none  [passed_along(): lax.ppermute(array, axis, [(i, (i + by) % size) for i in range(size)])]
    pallas_call x0 -> x8, Pallas kernels: none -> 111 us  [the longest x1 29.3 us: exchange_positions(): pl.pallas_call(kernel, out_shape=jax.ShapeDtypeStruct((count, 16, 128), F...]
    reduce_scatter x1 -> x0, waiting for transfers between devices: 65 us -> none  [body(): lax.psum_scatter(first + jnp.einsum('ax,nmxc->anmc', inverse_sin, sigma_h...]
    all_gather x1 -> x0, waiting for transfers between devices: 42.7 us -> none  [body(): full_rows = lax.all_gather(green, 'bos', axis=3, tiled=True)]
    dot_general x9 -> x0, matrix products: 39.4 us -> none  [the longest x3 12.9 us: row_step(): return jnp.einsum('...c,cd->...d', field, matrix, precision=HIGHEST)]
    reduce_sum x8 -> x0, other arithmetic: 27.1 us -> none  [body(): real_part = jnp.sum(green_re * weight_re - green_im * weight_im, axis=2)]
    mul x16 -> x0, local copies, waits for them, and re-layouts: 24.8 us -> none  [body(): real_part = jnp.sum(green_re * weight_re - green_im * weight_im, axis=2)]
    ppermute x5 -> x0, starting transfers between devices: 21.5 us -> none  [passed_along(): lax.ppermute(array, axis, [(i, (i + by) % size) for i in range(size)])]
  transfers between devices with their start and end apart: 7 -> 0, of which waited for: 7 -> 0; matrix products, arithmetic and copies ran while one was open for 3% -> 0% of each run, Pallas kernels for 0% -> 0%
where the time goes in v1:
time: 114 us
  Pallas kernels  111 us (97%)
  local copies, waits for them, and re-layouts  2.24 us (2%)
    pallas_call x1, Pallas kernels, exchange_positions(): pl.pallas_call(kernel, out_shape=jax.ShapeDtypeStruct((count, 16, 128), F...  29.3 us
    pallas_call x2, Pallas kernels, exchange_axis(): pl.pallas_call(kernel, out_shape=jax.ShapeDtypeStruct(out_shape, F32), in...  27.4 us
    pallas_call x1, Pallas kernels, contract(): pl.pallas_call(kernel, out_shape=jax.ShapeDtypeStruct((2, 3, 64, 128), F3...  23.8 us
    pallas_call x1, Pallas kernels, exchange_green(): pl.pallas_call(kernel, out_shape=(jax.ShapeDtypeStruct((2, 9, BOS, 4, 128...  20.7 us
    pallas_call x1, Pallas kernels, to_positions(): pl.pallas_call(kernel, out_shape=jax.ShapeDtypeStruct((L, 2, 16, 128), F3...  4.66 us
    pallas_call x1, Pallas kernels, back_y(): pl.pallas_call(kernel, out_shape=jax.ShapeDtypeStruct((4, 9, 8, 128), F32...  2.48 us
    pallas_call x1, Pallas kernels, back_x(): pl.pallas_call(kernel, out_shape=jax.ShapeDtypeStruct((BOS, 8, 384), F32)...  2.4 us

profile of v1, /device:TPU:1, one launch (start us, length us, event | category | flops | bytes accessed | tf_op | source)
XLA Modules:
  0.0 113.6 jit_solution(5132486888734351497)
XLA Ops:
  0.0 0.0 copy-start
  0.0 20.7 %exchange_green.1 = (bf16[2,9,16,4,128]{4,3,2,1,0:T(4,128)(2,1)}, f32[16,8,8]{2,1,0:T(8,128)}) custom-call(bf16[2,2,8,9,4,128]{5,4,3,2,1,0:T(4,128)(2,1)} %bitcast.9, f32[8,8]{1,0:T(8,128)} %v_ref.1), custom_call_target="tpu_custom_call" | custom-call | tf_op jit(solution)/shard_map/exchange_green/pallas_call | solution.py:127
  20.7 0.9 copy.13
  21.6 0.1 reshape.18
  21.7 0.1 rev.3
  21.7 0.5 constant_dynamic-slice_fusion.v_ref
  22.3 0.0 copy-done
  22.3 0.7 constant_dynamic-slice_fusion.1
  22.9 4.7 %to_positions.1 = f32[64,2,16,128]{3,2,1,0:T(8,128)} custom-call(bf16[2,9,64,128]{3,2,1,0:T(8,128)(2,1)} %bitcast.8, bf16[1,576,128]{2,1,0:T(8,128)(2,1)} %bitcast.7, f32[1,128]{1,0:T(1,128)} %constant_dynamic-slice_fusion.v_ref, bf16[2,128,128]{2,1,0:T(8,128)(2,1)} %constant.38.clone.g1, bf16[2,256,256]{2,1,0:T(8,128)(2,1)} %constant.39.clone.g2, ...), custom_call_target="tpu_custom_call" | custom-call | tf_op jit(solution)/shard_map/to_positions/pallas_call | solution.py:243
  27.6 29.3 %exchange_positions.1.r_ref = f32[128,16,128]{2,1,0:T(8,128)} custom-call(f32[128,16,128]{2,1,0:T(8,128)} %bitcast.6), custom_call_target="tpu_custom_call" | custom-call | tf_op jit(solution)/shard_map/exchange_positions/pallas_call | solution.py:176
  57.6 23.8 %contract.1.s_ref = f32[2,3,64,128]{3,2,1,0:T(8,128)} custom-call(s32[16]{0:T(128)} %bo.1, s32[1]{0:T(128)S(6)} %copy.14.ws, f32[128,16,128]{2,1,0:T(8,128)} %exchange_positions.1.r_ref), custom_call_target="tpu_custom_call" | custom-call | tf_op jit(solution)/shard_map/contract/pallas_call | solution.py:333
  81.4 12.5 %exchange_octets.1.b_ref = f32[8,2,3,8,128]{4,3,2,1,0:T(8,128)} custom-call(f32[2,3,64,128]{3,2,1,0:T(8,128)} %contract.1.s_ref), custom_call_target="tpu_custom_call" | custom-call | tf_op jit(solution)/shard_map/exchange_octets/pallas_call | solution.py:212
  93.9 2.4 %back_x.1.s_ref = f32[16,8,384]{2,1,0:T(8,128)} custom-call(f32[8,2,3,8,128]{4,3,2,1,0:T(8,128)} %exchange_octets.1.b_ref, bf16[2,3,128,512]{3,2,1,0:T(8,128)(2,1)} %constant.42.clone.m_ref), custom_call_target="tpu_custom_call" | custom-call | tf_op jit(solution)/shard_map/back_x/pallas_call | solution.py:368
  96.3 14.9 %exchange_rows.1.e_ref = f32[16,8,384]{2,1,0:T(8,128)} custom-call(f32[16,8,384]{2,1,0:T(8,128)} %back_x.1.s_ref), custom_call_target="tpu_custom_call" | custom-call | tf_op jit(solution)/shard_map/exchange_rows/pallas_call | solution.py:212
  111.2 2.5 %back_y.1 = f32[4,9,8,128]{3,2,1,0:T(8,128)} custom-call(f32[16,8,384]{2,1,0:T(8,128)} %exchange_rows.1.e_ref, bf16[2,512,512]{2,1,0:T(8,128)(2,1)} %constant.43.clone.m_ref), custom_call_target="tpu_custom_call" | custom-call | tf_op jit(solution)/shard_map/back_y/pallas_call | solution.py:394
Async XLA Ops:
  0.0 22.3 %copy-start = (bf16[8,9,64,128]{3,2,1,0:T(8,128)(2,1)S(1)}, bf16[8,9,64,128]{3,2,1,0:T(8,128)(2,1)}, u32[]{:S(2)}) copy-start(bf16[8,9,64,128]{3,2,1,0:T(8,128)(2,1)} %param.12) | copy-start | bytes 3538948

commit v2 on v1

--- a/solution.py
+++ b/solution.py
@@ -88,8 +88,20 @@
     return hi, (x - hi.astype(F32)).astype(BF16)
 
 
+def greet(axes):
+    barrier = pltpu.get_barrier_semaphore()
+    total = 0
+    for axis, size in axes:
+        me = lax.axis_index(axis)
+        for i in range(1, size):
+            pl.semaphore_signal(barrier, inc=1, device_id={axis: lax.rem(me + i, size)}, device_id_type=MESH)
+        total += size - 1
+    pl.semaphore_wait(barrier, total)
+
+
 def exchange_green(green, vertex):
     def kernel(g_ref, v_ref, x_ref, vo_ref, gs, gr, vs, vr, own):
+        greet([("bos", BOS)])
         me = lax.axis_index("bos")
         mine = [
             pltpu.make_async_copy(g_ref.at[:, me // 8, me % 8], x_ref.at[:, :, me], own.at[0]),
@@ -133,7 +145,7 @@
         in_specs=[any_, any_],
         out_specs=(any_, any_),
         scratch_shapes=[pltpu.SemaphoreType.DMA((BOS,))] * 4 + [pltpu.SemaphoreType.DMA((2,))],
-        compiler_params=pltpu.CompilerParams(has_side_effects=True),
+        compiler_params=pltpu.CompilerParams(has_side_effects=True, collective_id=0),
         name="exchange_green",
     )(green, vertex)
 
@@ -141,12 +153,16 @@
 def exchange_positions(sent):
     count = FER * BOS
 
-    def kernel(s_ref, r_ref, ss, rs, own):
+    def kernel(s_ref, r_ref, ss, rs, own, seen):
+        greet([("bos", BOS), ("fer", FER)])
         f, j = lax.axis_index("fer"), lax.axis_index("bos")
         me = j * FER + f
         row = count - 1 - ((j // 8) * 64 + f * 8 + lax.rem(j, 8))
         mine = pltpu.make_async_copy(s_ref.at[me], r_ref.at[row], own)
         mine.start()
+        for i in range(1, FER):
+            pl.semaphore_signal(seen, inc=1, device_id={"fer": lax.rem(f + i, FER)}, device_id_type=MESH)
+        pl.semaphore_wait(seen, FER - 1)
 
         def send(i, carry):
             to = lax.rem(me + i, count)
@@ -178,14 +194,15 @@
         out_shape=jax.ShapeDtypeStruct((count, 16, 128), F32),
         in_specs=[any_],
         out_specs=any_,
-        scratch_shapes=[pltpu.SemaphoreType.DMA] * 3,
-        compiler_params=pltpu.CompilerParams(has_side_effects=True, vmem_limit_bytes=VMEM_LIMIT),
+        scratch_shapes=[pltpu.SemaphoreType.DMA] * 3 + [pltpu.SemaphoreType.REGULAR],
+        compiler_params=pltpu.CompilerParams(has_side_effects=True, collective_id=1, vmem_limit_bytes=VMEM_LIMIT),
         name="exchange_positions",
     )(sent)
 
 
 def exchange_axis(sent, axis, size, pick, out_shape, name):
     def kernel(s_ref, r_ref, ss, rs, own):
+        greet([(axis, size)])
         me = lax.axis_index(axis)
         mine = pltpu.make_async_copy(pick(s_ref, me), r_ref.at[me], own)
         copies = []
@@ -215,7 +232,7 @@
         in_specs=[any_],
         out_specs=any_,
         scratch_shapes=[pltpu.SemaphoreType.DMA((size,))] * 2 + [pltpu.SemaphoreType.DMA],
-        compiler_params=pltpu.CompilerParams(has_side_effects=True),
+        compiler_params=pltpu.CompilerParams(has_side_effects=True, collective_id=2 if axis == "fer" else 3),
         name=name,
     )(sent)
 
@@ -251,11 +268,11 @@
 
 
 def contract(received, block_order, window_start):
-    def kernel(bo, ws, r_ref, o_ref, gt, wk, wb, vert, hh, hl):
+    def kernel(bo, ws, r_ref, o_ref, gt, wk, wb, vert, h0, h1, rows):
         s = ws[0]
         lane = lax.broadcasted_iota(jnp.int32, (128, 128), 1)
         for ac in range(9):
-            gt[ac] = pltpu.roll(r_ref[:, ac, :].T, s, axis=1)
+            gt[ac] = r_ref[:, ac, :].T
         for j in range(BOS):
             base = (1 - j // 8) * 64 + (7 - j % 8)
             to = pl.multiple_of(8 * (15 - bo[j]), 8)
@@ -276,9 +293,9 @@
                 )
                 for ri, part in enumerate((t, turned)):
                     hi, lo = halves(part)
-                    rows = slice((2 * c + ri) * 128, (2 * c + ri) * 128 + 128)
-                    wb[rg, rows, 0:128] = hi
-                    wb[rg, rows, 128:256] = lo
+                    at = slice((2 * c + ri) * 128, (2 * c + ri) * 128 + 128)
+                    wb[rg, at, 0:128] = hi
+                    wb[rg, at, 128:256] = lo
         lane8 = lax.broadcasted_iota(jnp.int32, (8, 128), 1)
         raw = [r_ref[8 * (7 - o) : 8 * (7 - o) + 8, 14, :] for o in range(8)]
         turned = [jnp.zeros((8, 128), F32) for _ in range(8)]
@@ -289,44 +306,40 @@
                 turned[o] = jnp.where(here, pltpu.roll(raw[o], by, axis=1), turned[o])
         for o in range(8):
             vert[8 * o : 8 * o + 8, :] = turned[o]
-        o_ref[...] = jnp.zeros_like(o_ref)
-
-        row8 = lax.broadcasted_iota(jnp.int32, (8, 128), 0)
-        back = s + row8
-        origin = (lane8 - back + 256) % 128
-        upper = [origin >= 128 - back - 8 * o for o in range(8)]
-
-        def skewed(ac, row):
-            y = jnp.broadcast_to(gt[ac, pl.ds(row, 1), :], (8, 128))
-            for bit in (1, 2, 4):
-                y = jnp.where(row8 & bit != 0, pltpu.roll(y, bit, axis=1), y)
-            return y
-
-        for rg in range(2):
-
-            def step(r16, carry):
-                r = rg * 16 + r16
+        lane16 = lax.broadcasted_iota(jnp.int32, (16, 128), 1)
+
+        def build(block, h_ref):
+            for vi in range(8):
+                by = s + (8 * block + vi)
+                upper = lane16 >= 128 - by
+                row = jnp.broadcast_to(vert[pl.ds(8 * block + vi, 1), :], (16, 128))
+                for rg in range(2):
+                    for a in range(3):
+                        for cr in range(6):
+                            ac, at = 3 * a + cr // 2, (cr % 2) * 32 + rg * 16
+                            y = jnp.where(upper, gt[ac, 64 + at : 80 + at, :], gt[ac, at : at + 16, :])
+                            hi, lo = halves(pltpu.roll(y, by, axis=1) * row)
+                            to = (vi * 3 + a) * 16
+                            h_ref[rg, to : to + 16, cr * 128 : cr * 128 + 128] = hi
+                            h_ref[rg, 384 + to : 400 + to, cr * 128 : cr * 128 + 128] = lo
+
+        def multiply(block, h_ref):
+            for rg in range(2):
+                acc = mm(h_ref[rg], wb[rg])
+                acc = acc[:384] + acc[384:]
+                rows[rg] = (acc[:, :128] + acc[:, 128:]).reshape(8, 48, 128)
                 for a in range(3):
-                    for c in range(3):
-                        for ri in range(2):
-                            first = skewed(3 * a + c, 64 + ri * 32 + r)
-                            second = skewed(3 * a + c, ri * 32 + r)
-                            octets = []
-                            for o in range(8):
-                                y = jnp.where(upper[o], first, second)
-                                octets.append(pltpu.roll(y, 8 * o, axis=1) if o else y)
-                            h = jnp.concatenate(octets, axis=0)
-                            hi, lo = halves(h * vert[...])
-                            at = (slice(64 * a, 64 * a + 64), slice((2 * c + ri) * 128, (2 * c + ri) * 128 + 128))
-                            hh[at] = hi
-                            hl[at] = lo
-                acc = mm(hh[...], wb[rg]) + mm(hl[...], wb[rg])
-                res = (acc[:, :128] + acc[:, 128:]).reshape(3, 64, 128)
-                here = lax.broadcasted_iota(jnp.int32, (3, 64, 128), 2) % 16 == r16
-                o_ref[rg] = jnp.where(here, res, o_ref[rg])
-                return carry
-
-            lax.fori_loop(0, 16, step, 0)
+                    out = jnp.zeros((8, 128), F32)
+                    for r16 in range(16):
+                        out = jnp.where(lane8 % 16 == r16, rows[rg, :, a * 16 + r16, :], out)
+                    o_ref[rg, a, pl.ds(8 * block, 8), :] = out
+
+        slots = (h0, h1)
+        build(0, h0)
+        for block in range(8):
+            if block < 7:
+                build(block + 1, slots[(block + 1) % 2])
+            multiply(block, slots[block % 2])
 
     vm = pl.BlockSpec(memory_space=pltpu.VMEM)
     sm = pl.BlockSpec(memory_space=pltpu.SMEM)
@@ -340,8 +353,9 @@
             pltpu.VMEM((5, 128, 128), F32),
             pltpu.VMEM((2, 768, 256), BF16),
             pltpu.VMEM((64, 128), F32),
-            pltpu.VMEM((192, 768), BF16),
-            pltpu.VMEM((192, 768), BF16),
+            pltpu.VMEM((2, 768, 768), BF16),
+            pltpu.VMEM((2, 768, 768), BF16),
+            pltpu.VMEM((2, 8, 48, 128), F32),
         ],
         compiler_params=pltpu.CompilerParams(vmem_limit_bytes=VMEM_LIMIT),
         name="contract",

time: 114 us -> 83.4 us (0.73)
  Pallas kernels: 111 us -> 80.1 us
    pallas_call x1, Pallas kernels: 23.8 us -> 11.5 us  [contract(): pl.pallas_call(kernel, out_shape=jax.ShapeDtypeStruct((2, 3, 64, 128), F3...]
    pallas_call x2, Pallas kernels: 27.4 us -> 18.3 us  [exchange_axis(): pl.pallas_call(kernel, out_shape=jax.ShapeDtypeStruct(out_shape, F32), in...]
    pallas_call x1, Pallas kernels: 20.7 us -> 13.4 us  [exchange_green(): pl.pallas_call(kernel, out_shape=(jax.ShapeDtypeStruct((2, 9, BOS, 4, 128...]
    pallas_call x1, Pallas kernels: 29.3 us -> 27.4 us  [exchange_positions(): pl.pallas_call(kernel, out_shape=jax.ShapeDtypeStruct((count, 16, 128), F...]
where the time goes in v2:
time: 83.4 us; the launch traced here: 83 us
  Pallas kernels  80.1 us (96%)
  local copies, waits for them, and re-layouts  2.24 us (3%)
    pallas_call x1, Pallas kernels, exchange_positions(): pl.pallas_call(kernel, out_shape=jax.ShapeDtypeStruct((count, 16, 128), F...  27.4 us
    pallas_call x2, Pallas kernels, exchange_axis(): pl.pallas_call(kernel, out_shape=jax.ShapeDtypeStruct(out_shape, F32), in...  18.3 us
    pallas_call x1, Pallas kernels, exchange_green(): pl.pallas_call(kernel, out_shape=(jax.ShapeDtypeStruct((2, 9, BOS, 4, 128...  13.4 us
    pallas_call x1, Pallas kernels, contract(): pl.pallas_call(kernel, out_shape=jax.ShapeDtypeStruct((2, 3, 64, 128), F3...  11.5 us
    pallas_call x1, Pallas kernels, to_positions(): pl.pallas_call(kernel, out_shape=jax.ShapeDtypeStruct((L, 2, 16, 128), F3...  4.66 us
    pallas_call x1, Pallas kernels, back_y(): pl.pallas_call(kernel, out_shape=jax.ShapeDtypeStruct((4, 9, 8, 128), F32...  2.48 us
    pallas_call x1, Pallas kernels, back_x(): pl.pallas_call(kernel, out_shape=jax.ShapeDtypeStruct((BOS, 8, 384), F32)...  2.4 us

profile of v2, /device:TPU:1, one launch (start us, length us, event | category | flops | bytes accessed | tf_op | source)
XLA Modules:
  0.0 83.0 jit_solution(14772823725938261281)
XLA Ops:
  0.0 0.0 copy-start
  0.0 13.4 %exchange_green.1 = (bf16[2,9,16,4,128]{4,3,2,1,0:T(4,128)(2,1)}, f32[16,8,8]{2,1,0:T(8,128)}) custom-call(bf16[2,2,8,9,4,128]{5,4,3,2,1,0:T(4,128)(2,1)} %bitcast.9, f32[8,8]{1,0:T(8,128)} %v_ref.1), custom_call_target="tpu_custom_call" | custom-call | tf_op jit(solution)/shard_map/exchange_green/pallas_call | solution.py:139
  13.4 0.9 %copy.13 = f32[8,16,8]{2,1,0:T(8,128)S(1)} copy(f32[8,16,8]{2,0,1:T(8,128)} %bitcast.10) | data formatting | bytes 8192 | tf_op jit(solution)/shard_map/transpose | solution.py:421
  14.2 0.1 reshape.18
  14.3 0.1 rev.3
  14.4 0.5 constant_dynamic-slice_fusion.v_ref
  14.9 0.0 copy-done
  14.9 0.7 constant_dynamic-slice_fusion.1
  15.6 4.7 %to_positions.1 = f32[64,2,16,128]{3,2,1,0:T(8,128)} custom-call(bf16[2,9,64,128]{3,2,1,0:T(8,128)(2,1)} %bitcast.8, bf16[1,576,128]{2,1,0:T(8,128)(2,1)} %bitcast.7, f32[1,128]{1,0:T(1,128)} %constant_dynamic-slice_fusion.v_ref, bf16[2,128,128]{2,1,0:T(8,128)(2,1)} %constant.38.clone.g1, bf16[2,256,256]{2,1,0:T(8,128)(2,1)} %constant.39.clone.g2, ...), custom_call_target="tpu_custom_call" | custom-call | tf_op jit(solution)/shard_map/to_positions/pallas_call | solution.py:260
  20.3 27.4 %exchange_positions.1.r_ref = f32[128,16,128]{2,1,0:T(8,128)} custom-call(f32[128,16,128]{2,1,0:T(8,128)} %bitcast.6), custom_call_target="tpu_custom_call" | custom-call | tf_op jit(solution)/shard_map/exchange_positions/pallas_call | solution.py:192
  48.3 11.5 %contract.1.s_ref = f32[2,3,64,128]{3,2,1,0:T(8,128)} custom-call(s32[16]{0:T(128)} %bo.1, s32[1]{0:T(128)S(6)} %copy.14.ws, f32[128,16,128]{2,1,0:T(8,128)} %exchange_positions.1.r_ref), custom_call_target="tpu_custom_call" | custom-call | tf_op jit(solution)/shard_map/contract/pallas_call | solution.py:346
  59.8 9.2 %exchange_octets.1.b_ref = f32[8,2,3,8,128]{4,3,2,1,0:T(8,128)} custom-call(f32[2,3,64,128]{3,2,1,0:T(8,128)} %contract.1.s_ref), custom_call_target="tpu_custom_call" | custom-call | tf_op jit(solution)/shard_map/exchange_octets/pallas_call | solution.py:229
  69.1 2.4 %back_x.1.s_ref = f32[16,8,384]{2,1,0:T(8,128)} custom-call(f32[8,2,3,8,128]{4,3,2,1,0:T(8,128)} %exchange_octets.1.b_ref, bf16[2,3,128,512]{3,2,1,0:T(8,128)(2,1)} %constant.42.clone.m_ref), custom_call_target="tpu_custom_call" | custom-call | tf_op jit(solution)/shard_map/back_x/pallas_call | solution.py:382
  71.5 9.1 %exchange_rows.1.e_ref = f32[16,8,384]{2,1,0:T(8,128)} custom-call(f32[16,8,384]{2,1,0:T(8,128)} %back_x.1.s_ref), custom_call_target="tpu_custom_call" | custom-call | tf_op jit(solution)/shard_map/exchange_rows/pallas_call | solution.py:229
  80.5 2.5 %back_y.1 = f32[4,9,8,128]{3,2,1,0:T(8,128)} custom-call(f32[16,8,384]{2,1,0:T(8,128)} %exchange_rows.1.e_ref, bf16[2,512,512]{2,1,0:T(8,128)(2,1)} %constant.43.clone.m_ref), custom_call_target="tpu_custom_call" | custom-call | tf_op jit(solution)/shard_map/back_y/pallas_call | solution.py:408
Async XLA Ops:
  0.0 14.9 %copy-start = (bf16[8,9,64,128]{3,2,1,0:T(8,128)(2,1)S(1)}, bf16[8,9,64,128]{3,2,1,0:T(8,128)(2,1)}, u32[]{:S(2)}) copy-start(bf16[8,9,64,128]{3,2,1,0:T(8,128)(2,1)} %param.12) | copy-start | bytes 3538948

commit v3 on v0

v3 whole, which is shorter than its diff:
```python
import functools
import math

import jax
import jax.numpy as jnp
import ml_dtypes
import numpy as np
from jax import lax
from jax.experimental import pallas as pl
from jax.experimental.pallas import tpu as pltpu
from jax.sharding import PartitionSpec as P

MESH = pl.DeviceIdType.MESH
BF16 = jnp.bfloat16
F32 = jnp.float32
L = 64
FER = 8
BOS = 16
VMEM_LIMIT = 56 * 1024 * 1024


def split_np(m):
    hi = m.astype(ml_dtypes.bfloat16)
    lo = (m - hi.astype(np.float64)).astype(ml_dtypes.bfloat16)
    return np.stack([hi, lo])


def trig(a, b):
    t = 2.0 * math.pi * ((np.asarray(a)[:, None] * np.asarray(b)[None, :]) % L) / L
    return np.cos(t), np.sin(t)


def complex_map(c, s, sign):
    m = np.zeros((2, 2) + c.shape)
    m[0, 0], m[1, 1] = c, c
    m[1, 0], m[0, 1] = -sign * s, sign * s
    return m


def first_matrix(sign, scale):
    c, s = trig(np.arange(L), np.arange(L))
    m = complex_map(c, s, sign) * scale
    return split_np(m.transpose(1, 3, 0, 2).reshape(2 * L, 2 * L))


def second_matrix(sign, scale, grouped):
    c, s = trig(np.arange(L), np.arange(L))
    m = complex_map(c, s, sign) * scale
    m = m.reshape(2, 2, L, 2, 2, 16)
    full = np.zeros((2, 2, L, 2, 2, 2, 2, 16))
    for pair in range(2):
        full[:, pair, :, :, :, pair] = m.transpose(0, 2, 3, 4, 1, 5)
    if not grouped:
        full = full.transpose(0, 1, 2, 3, 5, 6, 4, 7)
    return split_np(full.reshape(4 * L, 4 * L))


def out_x_matrix():
    c, s = trig(np.arange(L), np.arange(L))
    m = complex_map(c, s, 1.0) * (-1.0 / L)
    m = m.reshape(2, 2, 2, 2, 16, 16, 4)
    full = np.zeros((3, 16, 2, 4, 2, 2, 4, 2, 16))
    for b in range(3):
        full[b, :, :, :, :, :, b] = m.transpose(5, 1, 6, 2, 3, 0, 4)
    return split_np(full.reshape(3, 128, 512))


def out_y_matrix():
    c, s = trig(np.arange(L), np.arange(L))
    m = complex_map(c, s, 1.0) / L
    m = m.reshape(2, 2, 16, 4, L)
    full = np.zeros((4, 16, 2, 4, 4, 2, L))
    for k in range(4):
        full[:, :, :, k, k] = m.transpose(3, 2, 0, 1, 4)
    return split_np(full.reshape(512, 512))


def mm(a, b):
    return jnp.dot(a, b, preferred_element_type=F32)


def nt(a, b):
    return lax.dot_general(a, b, (((1,), (1,)), ((), ())), preferred_element_type=F32)


def halves(x):
    hi = x.astype(BF16)
    return hi, (x - hi.astype(F32)).astype(BF16)


def ring(axis, size, start):
    me = lax.axis_index(axis)
    copies = []
    for i in range(1, size):
        to = lax.rem(me + i, size)
        copies.append(
            pltpu.make_async_remote_copy(device_id={axis: to}, device_id_type=MESH, **start(to, i))
        )
    return copies


def transform(x, m1, m2, s_ref, row):
    z = nt(m1[0], x) + nt(m1[1], x)
    hi, lo = halves(jnp.concatenate([z[:L], z[L:]], axis=1))
    y = mm(hi, m2[0]) + mm(hi, m2[1]) + mm(lo, m2[0])
    for half in range(2):
        s_ref[:, half, row, :] = y[:, half * 128 : half * 128 + 128]


def whole_kernel(
    bo, ws, green, weight, vertex, g1h, g2h, w1h, w2h, mxh, myh, out,
    g1, g2, w1, w2, mx, my, planes, vsend, vgot, vsum, sg, sw, rg_in, rw_in,
    gt, wk, wb, vert, h0, h1, rows, octets, b_in, lh, ll, quads, e_in, yh, yl,
    csem, green_s, green_r, vert_s, vert_r, pos_s, pos_r, own, oct_s, oct_r, quad_s, quad_r, seen,
):
    f, j = lax.axis_index("fer"), lax.axis_index("bos")
    me = j * FER + f
    place = (j // 8) * 64 + f * 8 + lax.rem(j, 8)
    count = FER * BOS

    barrier = pltpu.get_barrier_semaphore()
    for axis, size, mine in (("bos", BOS, j), ("fer", FER, f)):
        for i in range(1, size):
            pl.semaphore_signal(
                barrier, inc=1, device_id={axis: lax.rem(mine + i, size)}, device_id_type=MESH
            )
    loads = [
        pltpu.make_async_copy(a, b, csem.at[i])
        for i, (a, b) in enumerate(
            ((w1h, w1), (w2h, w2), (g1h, g1), (g2h, g2), (mxh, mx), (myh, my))
        )
    ]
    for c in loads:
        c.start()

    loads[0].wait()
    loads[1].wait()
    for k in range(5):
        if k < 4:
            x = weight[f, 128 * k : 128 * k + 128]
        else:
            x = jnp.concatenate([weight[f, 512:576], jnp.zeros((64, 128), BF16)], axis=0)
        transform(x, w1, w2, sw, k)
    lane8 = lax.broadcasted_iota(jnp.int32, (8, 128), 1)
    spread = jnp.concatenate([vertex[...]] * BOS, axis=1)
    vsend[...] = jnp.where(lane8 // 8 == bo[j], spread, 0.0)

    pl.semaphore_wait(barrier, BOS + FER - 2)
    for i in range(1, FER):
        pl.semaphore_signal(seen, inc=1, device_id={"fer": lax.rem(f + i, FER)}, device_id_type=MESH)

    near = ring(
        "bos", BOS,
        lambda to, i: dict(
            src_ref=green.at[:, to // 8, lax.rem(to, 8)], dst_ref=planes.at[:, :, j],
            send_sem=green_s.at[i], recv_sem=green_r.at[i],
        ),
    )
    near += ring(
        "bos", BOS,
        lambda to, i: dict(
            src_ref=vsend, dst_ref=vgot.at[j], send_sem=vert_s.at[i], recv_sem=vert_r.at[i]
        ),
    )
    for c in near:
        c.start()
    kept = pltpu.make_async_copy(green.at[:, j // 8, lax.rem(j, 8)], planes.at[:, :, j], own.at[0])
    kept.start()
    vgot[j] = vsend[...]

    pl.semaphore_wait(seen, FER - 1)

    def everywhere(src, dst, which):
        mine = pltpu.make_async_copy(src.at[me // 2, lax.rem(me, 2)], dst.at[place], own.at[1 + which])
        mine.start()

        def send(i, carry):
            to = lax.rem(me + i, count)
            pltpu.make_async_remote_copy(
                src_ref=src.at[to // 2, lax.rem(to, 2)],
                dst_ref=dst.at[place],
                send_sem=pos_s.at[which],
                recv_sem=pos_r.at[which],
                device_id={"fer": lax.rem(to, FER), "bos": to // FER},
                device_id_type=MESH,
            ).start()
            return carry

        lax.fori_loop(1, count, send, 0)
        return mine

    def arrived(dst, which):
        part = dst.at[pl.ds(0, count - 1)]
        pltpu.make_async_remote_copy(
            src_ref=part, dst_ref=part, send_sem=pos_s.at[which], recv_sem=pos_r.at[which],
            device_id={"bos": lax.rem(j + 1, BOS)}, device_id_type=MESH,
        ).wait()

    mine_w = everywhere(sw, rw_in, 0)

    kept.wait()
    for c in near:
        c.wait()
    total = vgot[0]
    for i in range(1, BOS):
        total = total + vgot[i]
    vsum[...] = total
    sg[:, :, 9, :] = jnp.broadcast_to(
        vsum[pl.ds(lax.rem(j, 8), 1), :].reshape(1, 1, 128), (L, 2, 128)
    )
    loads[2].wait()
    loads[3].wait()
    for ac in range(9):
        x = jnp.concatenate([planes[n2, ac].reshape(L, 128) for n2 in range(2)], axis=0)
        transform(x, g1, g2, sg, ac)
    mine_g = everywhere(sg, rg_in, 1)

    mine_w.wait()
    arrived(rw_in, 0)
    lane = lax.broadcasted_iota(jnp.int32, (128, 128), 1)
    sub = lax.broadcasted_iota(jnp.int32, (128, 128), 0)
    target = jnp.zeros((8, 128), jnp.int32)
    owner = (lane8 // 64) * 8 + lane8 % 8
    for i in range(BOS):
        target = jnp.where(owner == i, bo[i] * 8, target)
    target = target + lane8 // 8 % 8
    order = jnp.where(sub == jnp.concatenate([target] * 16, axis=0), 1.0, 0.0).astype(BF16)
    for k in range(5):
        hi, lo = halves(rw_in[:, k, :])
        wk[k] = mm(order, hi) + mm(order, lo)
    for rg in range(2):
        for c in range(3):
            t = jnp.zeros((128, 128), F32)
            for b in range(3):
                k, odd = divmod(3 * c + b, 2)
                by = (32 * b - 64 * rg - 32 * odd) % 128
                piece = pltpu.roll(wk[k], by, axis=1) if by else wk[k]
                t = jnp.where(lane // 32 == b, piece, t)
            turned = jnp.where(lane % 32 < 16, -pltpu.roll(t, 112, axis=1), pltpu.roll(t, 16, axis=1))
            for ri, part in enumerate((t, turned)):
                hi, lo = halves(part)
                at = slice((2 * c + ri) * 128, (2 * c + ri) * 128 + 128)
                wb[rg, at, 0:128] = hi
                wb[rg, at, 128:256] = lo

    mine_g.wait()
    arrived(rg_in, 1)
    for ac in range(9):
        gt[ac] = rg_in[:, ac, :].T
    vert[...] = rg_in[0:64, 9, :]

    s = ws[0]
    lane16 = lax.broadcasted_iota(jnp.int32, (16, 128), 1)

    def octet(t):
        return lax.rem(f + 1 + t, FER)

    def build(t, h_ref):
        base = 8 * octet(t)
        for vi in range(8):
            by = s + base + vi
            upper = lane16 >= by
            back = lax.rem(128 - by, 128)
            row = jnp.broadcast_to(vert[pl.ds(base + vi, 1), :], (16, 128))
            for rg in range(2):
                for a in range(3):
                    for cr in range(6):
                        ac, at = 3 * a + cr // 2, (cr % 2) * 32 + rg * 16
                        y = jnp.where(upper, gt[ac, at : at + 16, :], gt[ac, 64 + at : 80 + at, :])
                        hi, lo = halves(pltpu.roll(y, back, axis=1) * row)
                        to = (vi * 3 + a) * 16
                        h_ref[rg, to : to + 16, cr * 128 : cr * 128 + 128] = hi
                        h_ref[rg, 384 + to : 400 + to, cr * 128 : cr * 128 + 128] = lo

    def multiply(t, h_ref):
        for rg in range(2):
            acc = mm(h_ref[rg], wb[rg])
            acc = acc[:384] + acc[384:]
            rows[rg] = (acc[:, :128] + acc[:, 128:]).reshape(8, 48, 128)
            for a in range(3):
                o = jnp.zeros((8, 128), F32)
                for r16 in range(16):
                    o = jnp.where(lane8 % 16 == r16, rows[rg, :, a * 16 + r16, :], o)
                octets[t, rg, a] = o

    def pass_on(t):
        return pltpu.make_async_remote_copy(
            src_ref=octets.at[t], dst_ref=b_in.at[f],
            send_sem=oct_s.at[t], recv_sem=oct_r.at[t],
            device_id={"fer": octet(t)}, device_id_type=MESH,
        )

    build(0, h0)

    def pair(t, carry):
        build(2 * t + 1, h1)
        multiply(2 * t, h0)
        pass_on(2 * t).start()
        build(jnp.minimum(2 * t + 2, 7), h0)
        multiply(2 * t + 1, h1)

        @pl.when(t < 3)
        def _():
            pass_on(2 * t + 1).start()

        return carry

    lax.fori_loop(0, 4, pair, 0)
    b_in[f] = octets[7]
    for t in range(7):
        pass_on(t).wait()

    lh[96:, :] = jnp.zeros((32, 512), BF16)
    ll[96:, :] = jnp.zeros((32, 512), BF16)
    for ryl in range(4):
        for half in range(2):
            for rg in range(2):
                hi, lo = halves(b_in[2 * ryl + half, rg].reshape(24, 128))
                at = (
                    slice(24 * ryl, 24 * ryl + 24),
                    slice((2 * half + rg) * 128, (2 * half + rg) * 128 + 128),
                )
                lh[at] = hi
                ll[at] = lo
    loads[4].wait()
    for b in range(3):
        y = nt(mx[0, b], lh[...]) + nt(mx[0, b], ll[...]) + nt(mx[1, b], lh[...])
        quads[:, :, b * 128 : b * 128 + 128] = y.reshape(BOS, 8, 128)
    last = ring(
        "bos", BOS,
        lambda to, i: dict(
            src_ref=quads.at[to], dst_ref=e_in.at[j], send_sem=quad_s.at[i], recv_sem=quad_r.at[i]
        ),
    )
    for c in last:
        c.start()
    e_in[j] = quads[j]
    loads[5].wait()
    for c in last:
        c.wait()

    for b in range(3):
        hi, lo = halves(e_in[:, :, b * 128 : b * 128 + 128].reshape(128, 128).T)
        for ryl in range(4):
            at = (slice(24 * b, 24 * b + 24), slice(128 * ryl, 128 * ryl + 128))
            yh[at] = hi[24 * ryl : 24 * ryl + 24]
            yl[at] = lo[24 * ryl : 24 * ryl + 24]
    y = mm(yh[...], my[0]) + mm(yl[...], my[0]) + mm(yh[...], my[1])
    for b in range(3):
        for a in range(3):
            for k in range(4):
                out[k, 3 * a + b] = y[24 * b + 8 * a : 24 * b + 8 * a + 8, 128 * k : 128 * k + 128]


def body(green, bos_weight, vertex, block_order, window_start):
    mats = [
        first_matrix(-1.0, 1.0),
        second_matrix(-1.0, 1.0, False),
        first_matrix(1.0, 1.0 / L),
        second_matrix(1.0, 1.0 / L, True),
        out_x_matrix(),
        out_y_matrix(),
    ]
    vm = pl.BlockSpec(memory_space=pltpu.VMEM)
    sm = pl.BlockSpec(memory_space=pltpu.SMEM)
    hbm = pl.BlockSpec(memory_space=pl.ANY)
    dma = pltpu.SemaphoreType.DMA
    out = pl.pallas_call(
        whole_kernel,
        out_shape=jax.ShapeDtypeStruct((4, 9, 8, 128), F32),
        in_specs=[sm, sm, vm, vm, vm] + [hbm] * 6,
        out_specs=vm,
        scratch_shapes=[pltpu.VMEM(m.shape, BF16) for m in mats]
        + [
            pltpu.VMEM((2, 9, BOS, 4, 128), BF16),
            pltpu.VMEM((8, 128), F32),
            pltpu.VMEM((BOS, 8, 128), F32),
            pltpu.VMEM((8, 128), F32),
            pltpu.VMEM((L, 2, 10, 128), F32),
            pltpu.VMEM((L, 2, 5, 128), F32),
            pltpu.VMEM((128, 10, 128), F32),
            pltpu.VMEM((128, 5, 128), F32),
            pltpu.VMEM((9, 128, 128), F32),
            pltpu.VMEM((5, 128, 128), F32),
            pltpu.VMEM((2, 768, 256), BF16),
            pltpu.VMEM((64, 128), F32),
            pltpu.VMEM((2, 768, 768), BF16),
            pltpu.VMEM((2, 768, 768), BF16),
            pltpu.VMEM((2, 8, 48, 128), F32),
            pltpu.VMEM((FER, 2, 3, 8, 128), F32),
            pltpu.VMEM((FER, 2, 3, 8, 128), F32),
            pltpu.VMEM((128, 512), BF16),
            pltpu.VMEM((128, 512), BF16),
            pltpu.VMEM((BOS, 8, 384), F32),
            pltpu.VMEM((BOS, 8, 384), F32),
            pltpu.VMEM((72, 512), BF16),
            pltpu.VMEM((72, 512), BF16),
            dma((6,)), dma((BOS,)), dma((BOS,)), dma((BOS,)), dma((BOS,)), dma((2,)), dma((2,)), dma((3,)),
            dma((FER,)), dma((FER,)), dma((BOS,)), dma((BOS,)), pltpu.SemaphoreType.REGULAR,
        ],
        compiler_params=pltpu.CompilerParams(
            has_side_effects=True, collective_id=0, vmem_limit_bytes=VMEM_LIMIT
        ),
        name="dual_self_energy",
    )(
        block_order,
        window_start,
        green.reshape(2, 2, 8, 9, 4, 128),
        bos_weight.reshape(8, 576, 128),
        vertex,
        *[jnp.asarray(m) for m in (mats[0], mats[1], mats[2], mats[3], mats[4], mats[5])],
    )
    return out.transpose(0, 2, 1, 3)


def solution(mesh):
    return jax.shard_map(
        body,
        mesh=mesh,
        in_specs=(
            P(None, "fer", None, "bos", None),
            P("bos", None, None, None),
            P("fer", "bos"),
            P(),
            P(),
        ),
        out_specs=P("bos", "fer", None, None),
        check_vma=False,
    )
```

time: 771 us -> 52.7 us (0.07)
  waiting for transfers between devices: 586 us -> 0 us
  local copies, waits for them, and re-layouts: 55.9 us -> 1.58 us
  Pallas kernels: 0 us -> 50.3 us
  other arithmetic: 45.9 us -> 0 us
  matrix products: 39.4 us -> 0 us
  starting transfers between devices: 21.6 us -> 0 us
  between operations: 15.5 us -> 0.66 us
    ppermute x5 -> x0, waiting for transfers between devices: 478 us -> none  [passed_along(): lax.ppermute(array, axis, [(i, (i + by) % size) for i in range(size)])]
    reduce_scatter x1 -> x0, waiting for transfers between devices: 65 us -> none  [body(): lax.psum_scatter(first + jnp.einsum('ax,nmxc->anmc', inverse_sin, sigma_h...]
    pallas_call x0 -> x1, Pallas kernels: none -> 50.3 us  [body(): pl.pallas_call(whole_kernel, out_shape=jax.ShapeDtypeStruct((4, 9, 8, 128...]
    all_gather x1 -> x0, waiting for transfers between devices: 42.7 us -> none  [body(): full_rows = lax.all_gather(green, 'bos', axis=3, tiled=True)]
    dot_general x9 -> x0, matrix products: 39.4 us -> none  [the longest x3 12.9 us: row_step(): return jnp.einsum('...c,cd->...d', field, matrix, precision=HIGHEST)]
    reduce_sum x8 -> x0, other arithmetic: 27.1 us -> none  [body(): real_part = jnp.sum(green_re * weight_re - green_im * weight_im, axis=2)]
    mul x16 -> x0, local copies, waits for them, and re-layouts: 24.8 us -> none  [body(): real_part = jnp.sum(green_re * weight_re - green_im * weight_im, axis=2)]
    ppermute x5 -> x0, starting transfers between devices: 21.5 us -> none  [passed_along(): lax.ppermute(array, axis, [(i, (i + by) % size) for i in range(size)])]
  transfers between devices with their start and end apart: 7 -> 0, of which waited for: 7 -> 0; matrix products, arithmetic and copies ran while one was open for 3% -> 0% of each run, Pallas kernels for 0% -> 0%
where the time goes in v3:
time: 52.7 us; the launch traced here: 52.5 us
  Pallas kernels  50.3 us (95%)
  local copies, waits for them, and re-layouts  1.58 us (3%)
  between operations  0.66 us (1%)
    pallas_call x1, Pallas kernels, body(): pl.pallas_call(whole_kernel, out_shape=jax.ShapeDtypeStruct((4, 9, 8, 128...  50.3 us
    unnamed x1, local copies, waits for them, and re-layouts  1.58 us

profile of v3, /device:TPU:1, one launch (start us, length us, event | category | flops | bytes accessed | tf_op | source)
XLA Modules:
  0.0 52.5 jit_solution(7280839004670685967)
XLA Ops:
  0.7 50.3 %dual_self_energy.1 = f32[4,9,8,128]{3,2,1,0:T(8,128)} custom-call(s32[16]{0:T(128)} %bo.1, s32[1]{0:T(128)S(6)} %copy.13.ws, bf16[2,2,8,9,4,128]{5,4,3,2,1,0:T(4,128)(2,1)} %bitcast.5, bf16[8,576,128]{2,1,0:T(8,128)(2,1)} %bitcast.3, f32[8,8]{1,0:T(8,128)} %vertex.1, bf16[2,128,128]{2,1,0:T(8,128)(2,1)} %constant.12.clone.g1h, ...), custom_call_target="tpu_custom_call" | custom-call | tf_op jit(solution)/shard_map/dual_self_energy/pallas_call | solution.py:368
  50.9 1.6 %copy.14 = f32[4,8,9,128]{3,1,2,0:T(8,128)} copy(f32[4,8,9,128]{3,1,2,0:T(8,128)} %bitcast.4) | data formatting | bytes 294912

commit v4 on v3

--- a/solution.py
+++ b/solution.py
@@ -88,6 +88,17 @@
     return hi, (x - hi.astype(F32)).astype(BF16)
 
 
+def hops(offset):
+    return sum(min(d, 4 - d) for d in offset[:3]) + 0.5 * offset[3]
+
+
+FAR_FIRST = sorted(
+    [(z, y, x, c) for z in range(4) for y in range(4) for x in range(4) for c in range(2)][1:],
+    key=hops,
+    reverse=True,
+)
+
+
 def ring(axis, size, start):
     me = lax.axis_index(axis)
     copies = []
@@ -109,7 +120,7 @@
 
 def whole_kernel(
     bo, ws, green, weight, vertex, g1h, g2h, w1h, w2h, mxh, myh, out,
-    g1, g2, w1, w2, mx, my, planes, vsend, vgot, vsum, sg, sw, rg_in, rw_in,
+    g1, g2, w1, w2, mx, my, planes, vsend, vgot, vsum, sa, sb, sw, ra_in, rb_in, rw_in,
     gt, wk, wb, vert, h0, h1, rows, octets, b_in, lh, ll, quads, e_in, yh, yl,
     csem, green_s, green_r, vert_s, vert_r, pos_s, pos_r, own, oct_s, oct_r, quad_s, quad_r, seen,
 ):
@@ -149,20 +160,25 @@
     for i in range(1, FER):
         pl.semaphore_signal(seen, inc=1, device_id={"fer": lax.rem(f + i, FER)}, device_id_type=MESH)
 
-    near = ring(
-        "bos", BOS,
-        lambda to, i: dict(
-            src_ref=green.at[:, to // 8, lax.rem(to, 8)], dst_ref=planes.at[:, :, j],
-            send_sem=green_s.at[i], recv_sem=green_r.at[i],
-        ),
-    )
-    near += ring(
+    parts = (pl.ds(0, 5), pl.ds(5, 4))
+    near = [
+        ring(
+            "bos", BOS,
+            lambda to, i, h=h: dict(
+                src_ref=green.at[:, to // 8, lax.rem(to, 8), parts[h]],
+                dst_ref=planes.at[:, parts[h], j],
+                send_sem=green_s.at[h, i], recv_sem=green_r.at[h, i],
+            ),
+        )
+        for h in range(2)
+    ]
+    near[1] += ring(
         "bos", BOS,
         lambda to, i: dict(
             src_ref=vsend, dst_ref=vgot.at[j], send_sem=vert_s.at[i], recv_sem=vert_r.at[i]
         ),
     )
-    for c in near:
+    for c in near[0] + near[1]:
         c.start()
     kept = pltpu.make_async_copy(green.at[:, j // 8, lax.rem(j, 8)], planes.at[:, :, j], own.at[0])
     kept.start()
@@ -174,19 +190,20 @@
         mine = pltpu.make_async_copy(src.at[me // 2, lax.rem(me, 2)], dst.at[place], own.at[1 + which])
         mine.start()
 
-        def send(i, carry):
-            to = lax.rem(me + i, count)
+        for dz, dy, dx, dc in FAR_FIRST:
+            x = lax.rem(lax.rem(j // 2, 4) + dx, 4)
+            y = lax.rem(lax.rem(f, 2) * 2 + j // 8 + dy, 4)
+            z = lax.rem(f // 2 + dz, 4)
+            fi = z * 2 + y // 2
+            ji = lax.rem(y, 2) * 8 + x * 2 + lax.rem(lax.rem(j, 2) + dc, 2)
             pltpu.make_async_remote_copy(
-                src_ref=src.at[to // 2, lax.rem(to, 2)],
+                src_ref=src.at[ji * 4 + fi // 2, lax.rem(fi, 2)],
                 dst_ref=dst.at[place],
                 send_sem=pos_s.at[which],
                 recv_sem=pos_r.at[which],
-                device_id={"fer": lax.rem(to, FER), "bos": to // FER},
+                device_id={"fer": fi, "bos": ji},
                 device_id_type=MESH,
             ).start()
-            return carry
-
-        lax.fori_loop(1, count, send, 0)
         return mine
 
     def arrived(dst, which):
@@ -199,21 +216,29 @@
     mine_w = everywhere(sw, rw_in, 0)
 
     kept.wait()
-    for c in near:
+    loads[2].wait()
+    loads[3].wait()
+
+    def planes_of(ac):
+        return jnp.concatenate([planes[n2, ac].reshape(L, 128) for n2 in range(2)], axis=0)
+
+    for c in near[0]:
+        c.wait()
+    for ac in range(5):
+        transform(planes_of(ac), g1, g2, sa, ac)
+    mine_a = everywhere(sa, ra_in, 1)
+    for c in near[1]:
         c.wait()
     total = vgot[0]
     for i in range(1, BOS):
         total = total + vgot[i]
     vsum[...] = total
-    sg[:, :, 9, :] = jnp.broadcast_to(
+    sb[:, :, 4, :] = jnp.broadcast_to(
         vsum[pl.ds(lax.rem(j, 8), 1), :].reshape(1, 1, 128), (L, 2, 128)
     )
-    loads[2].wait()
-    loads[3].wait()
-    for ac in range(9):
-        x = jnp.concatenate([planes[n2, ac].reshape(L, 128) for n2 in range(2)], axis=0)
-        transform(x, g1, g2, sg, ac)
-    mine_g = everywhere(sg, rg_in, 1)
+    for ac in range(5, 9):
+        transform(planes_of(ac), g1, g2, sb, ac - 5)
+    mine_b = everywhere(sb, rb_in, 2)
 
     mine_w.wait()
     arrived(rw_in, 0)
@@ -243,17 +268,23 @@
                 wb[rg, at, 0:128] = hi
                 wb[rg, at, 128:256] = lo
 
-    mine_g.wait()
-    arrived(rg_in, 1)
-    for ac in range(9):
-        gt[ac] = rg_in[:, ac, :].T
-    vert[...] = rg_in[0:64, 9, :]
+    mine_a.wait()
+    arrived(ra_in, 1)
+    for ac in range(5):
+        gt[ac] = ra_in[:, ac, :].T
+    mine_b.wait()
+    arrived(rb_in, 2)
+    for ac in range(5, 9):
+        gt[ac] = rb_in[:, ac - 5, :].T
+    vert[...] = rb_in[0:64, 4, :]
 
     s = ws[0]
     lane16 = lax.broadcasted_iota(jnp.int32, (16, 128), 1)
 
     def octet(t):
-        return lax.rem(f + 1 + t, FER)
+        u = lax.rem(t, 4)
+        dz = jnp.where(u == 3, 0, jnp.where(u == 2, 3, 2 - u))
+        return lax.rem(f // 2 + dz, 4) * 2 + lax.rem(f + 1 + t // 4, 2)
 
     def build(t, h_ref):
         base = 8 * octet(t)
@@ -376,9 +407,11 @@
             pltpu.VMEM((8, 128), F32),
             pltpu.VMEM((BOS, 8, 128), F32),
             pltpu.VMEM((8, 128), F32),
-            pltpu.VMEM((L, 2, 10, 128), F32),
             pltpu.VMEM((L, 2, 5, 128), F32),
-            pltpu.VMEM((128, 10, 128), F32),
+            pltpu.VMEM((L, 2, 5, 128), F32),
+            pltpu.VMEM((L, 2, 5, 128), F32),
+            pltpu.VMEM((128, 5, 128), F32),
+            pltpu.VMEM((128, 5, 128), F32),
             pltpu.VMEM((128, 5, 128), F32),
             pltpu.VMEM((9, 128, 128), F32),
             pltpu.VMEM((5, 128, 128), F32),
@@ -395,7 +428,7 @@
             pltpu.VMEM((BOS, 8, 384), F32),
             pltpu.VMEM((72, 512), BF16),
             pltpu.VMEM((72, 512), BF16),
-            dma((6,)), dma((BOS,)), dma((BOS,)), dma((BOS,)), dma((BOS,)), dma((2,)), dma((2,)), dma((3,)),
+            dma((6,)), dma((2, BOS)), dma((2, BOS)), dma((BOS,)), dma((BOS,)), dma((3,)), dma((3,)), dma((4,)),
             dma((FER,)), dma((FER,)), dma((BOS,)), dma((BOS,)), pltpu.SemaphoreType.REGULAR,
         ],
         compiler_params=pltpu.CompilerParams(

time: 52.7 us -> 49.2 us (0.934)
  Pallas kernels: 50.3 us -> 46.7 us
    pallas_call x1, Pallas kernels: 50.3 us -> 46.7 us  [body(): pl.pallas_call(whole_kernel, out_shape=jax.ShapeDtypeStruct((4, 9, 8, 128...]
where the time goes in v4:
time: 49.2 us; the launch traced here: 49 us
  Pallas kernels  46.7 us (95%)
  local copies, waits for them, and re-layouts  1.58 us (3%)
  between operations  0.66 us (1%)
    pallas_call x1, Pallas kernels, body(): pl.pallas_call(whole_kernel, out_shape=jax.ShapeDtypeStruct((4, 9, 8, 128...  46.7 us
    unnamed x1, local copies, waits for them, and re-layouts  1.58 us

profile of v4, /device:TPU:1, one launch (start us, length us, event | category | flops | bytes accessed | tf_op | source)
XLA Modules:
  0.0 49.0 jit_solution(3656478167558701129)
XLA Ops:
  0.7 46.7 %dual_self_energy.1 = f32[4,9,8,128]{3,2,1,0:T(8,128)} custom-call(s32[16]{0:T(128)} %bo.1, s32[1]{0:T(128)S(6)} %copy.13.ws, bf16[2,2,8,9,4,128]{5,4,3,2,1,0:T(4,128)(2,1)} %bitcast.5, bf16[8,576,128]{2,1,0:T(8,128)(2,1)} %bitcast.3, f32[8,8]{1,0:T(8,128)} %vertex.1, bf16[2,128,128]{2,1,0:T(8,128)(2,1)} %constant.12.clone.g1h, ...), custom_call_target="tpu_custom_call" | custom-call | tf_op jit(solution)/shard_map/dual_self_energy/pallas_call | solution.py:399
  47.4 1.6 %copy.14 = f32[4,8,9,128]{3,1,2,0:T(8,128)} copy(f32[4,8,9,128]{3,1,2,0:T(8,128)} %bitcast.4) | data formatting | bytes 294912

commit v5 on v4

--- a/solution.py
+++ b/solution.py
@@ -160,7 +160,7 @@
     for i in range(1, FER):
         pl.semaphore_signal(seen, inc=1, device_id={"fer": lax.rem(f + i, FER)}, device_id_type=MESH)
 
-    parts = (pl.ds(0, 5), pl.ds(5, 4))
+    parts = (pl.ds(0, 3), pl.ds(3, 6))
     near = [
         ring(
             "bos", BOS,
@@ -172,7 +172,7 @@
         )
         for h in range(2)
     ]
-    near[1] += ring(
+    near[0] += ring(
         "bos", BOS,
         lambda to, i: dict(
             src_ref=vsend, dst_ref=vgot.at[j], send_sem=vert_s.at[i], recv_sem=vert_r.at[i]
@@ -224,20 +224,20 @@
 
     for c in near[0]:
         c.wait()
-    for ac in range(5):
+    total = vgot[0]
+    for i in range(1, BOS):
+        total = total + vgot[i]
+    vsum[...] = total
+    sa[:, :, 3, :] = jnp.broadcast_to(
+        vsum[pl.ds(lax.rem(j, 8), 1), :].reshape(1, 1, 128), (L, 2, 128)
+    )
+    for ac in range(3):
         transform(planes_of(ac), g1, g2, sa, ac)
     mine_a = everywhere(sa, ra_in, 1)
     for c in near[1]:
         c.wait()
-    total = vgot[0]
-    for i in range(1, BOS):
-        total = total + vgot[i]
-    vsum[...] = total
-    sb[:, :, 4, :] = jnp.broadcast_to(
-        vsum[pl.ds(lax.rem(j, 8), 1), :].reshape(1, 1, 128), (L, 2, 128)
-    )
-    for ac in range(5, 9):
-        transform(planes_of(ac), g1, g2, sb, ac - 5)
+    for ac in range(3, 9):
+        transform(planes_of(ac), g1, g2, sb, ac - 3)
     mine_b = everywhere(sb, rb_in, 2)
 
     mine_w.wait()
@@ -249,69 +249,74 @@
     for i in range(BOS):
         target = jnp.where(owner == i, bo[i] * 8, target)
     target = target + lane8 // 8 % 8
-    order = jnp.where(sub == jnp.concatenate([target] * 16, axis=0), 1.0, 0.0).astype(BF16)
-    for k in range(5):
-        hi, lo = halves(rw_in[:, k, :])
-        wk[k] = mm(order, hi) + mm(order, lo)
-    for rg in range(2):
-        for c in range(3):
-            t = jnp.zeros((128, 128), F32)
-            for b in range(3):
-                k, odd = divmod(3 * c + b, 2)
-                by = (32 * b - 64 * rg - 32 * odd) % 128
-                piece = pltpu.roll(wk[k], by, axis=1) if by else wk[k]
-                t = jnp.where(lane // 32 == b, piece, t)
-            turned = jnp.where(lane % 32 < 16, -pltpu.roll(t, 112, axis=1), pltpu.roll(t, 16, axis=1))
-            for ri, part in enumerate((t, turned)):
-                hi, lo = halves(part)
-                at = slice((2 * c + ri) * 128, (2 * c + ri) * 128 + 128)
-                wb[rg, at, 0:128] = hi
-                wb[rg, at, 128:256] = lo
-
-    mine_a.wait()
-    arrived(ra_in, 1)
-    for ac in range(5):
-        gt[ac] = ra_in[:, ac, :].T
-    mine_b.wait()
-    arrived(rb_in, 2)
-    for ac in range(5, 9):
-        gt[ac] = rb_in[:, ac - 5, :].T
-    vert[...] = rb_in[0:64, 4, :]
+    target = jnp.concatenate([target] * 16, axis=0)
+    for par in range(2):
+        order = jnp.where((sub ^ par) == target, 1.0, 0.0).astype(BF16)
+        for k in range(5):
+            hi, lo = halves(rw_in[:, k, :])
+            wk[par, k] = mm(order, hi) + mm(order, lo)
+    for par in range(2):
+        for rg in range(2):
+            for c in range(3):
+                t = jnp.zeros((128, 128), F32)
+                for b in range(3):
+                    k, odd = divmod(3 * c + b, 2)
+                    by = (32 * b - 64 * rg - 32 * odd) % 128
+                    piece = pltpu.roll(wk[par, k], by, axis=1) if by else wk[par, k]
+                    t = jnp.where(lane // 32 == b, piece, t)
+                turned = jnp.where(lane % 32 < 16, -pltpu.roll(t, 112, axis=1), pltpu.roll(t, 16, axis=1))
+                for ri, part in enumerate((t, turned)):
+                    hi, lo = halves(part)
+                    at = slice((2 * c + ri) * 128, (2 * c + ri) * 128 + 128)
+                    wb[par, rg, at, 0:128] = hi
+                    wb[par, rg, at, 128:256] = lo
 
     s = ws[0]
     lane16 = lax.broadcasted_iota(jnp.int32, (16, 128), 1)
+    odd16 = lane16 % 2 == 1
 
     def octet(t):
         u = lax.rem(t, 4)
         dz = jnp.where(u == 3, 0, jnp.where(u == 2, 3, 2 - u))
         return lax.rem(f // 2 + dz, 4) * 2 + lax.rem(f + 1 + t // 4, 2)
 
-    def build(t, h_ref):
-        base = 8 * octet(t)
-        for vi in range(8):
-            by = s + base + vi
-            upper = lane16 >= by
-            back = lax.rem(128 - by, 128)
-            row = jnp.broadcast_to(vert[pl.ds(base + vi, 1), :], (16, 128))
+    def build(units, h_ref):
+        for n, (t, a) in enumerate(units):
+            base = 8 * octet(t)
+            shifts = [s + base + 2 * u for u in range(5)]
+            upper = [lane16 >= by for by in shifts]
+            back = [lax.rem(128 - by, 128) for by in shifts]
+            row = [
+                jnp.broadcast_to(vert[vi % 2, pl.ds(base + vi, 1), :], (16, 128)) for vi in range(8)
+            ]
             for rg in range(2):
-                for a in range(3):
-                    for cr in range(6):
-                        ac, at = 3 * a + cr // 2, (cr % 2) * 32 + rg * 16
-                        y = jnp.where(upper, gt[ac, at : at + 16, :], gt[ac, 64 + at : 80 + at, :])
-                        hi, lo = halves(pltpu.roll(y, back, axis=1) * row)
-                        to = (vi * 3 + a) * 16
-                        h_ref[rg, to : to + 16, cr * 128 : cr * 128 + 128] = hi
-                        h_ref[rg, 384 + to : 400 + to, cr * 128 : cr * 128 + 128] = lo
-
-    def multiply(t, h_ref):
+                for cr in range(6):
+                    ac, at = 3 * a + cr // 2, (cr % 2) * 32 + rg * 16
+                    low, high = gt[ac, at : at + 16, :], gt[ac, 64 + at : 80 + at, :]
+                    tile = [
+                        pltpu.roll(jnp.where(upper[u], low, high), back[u], axis=1) for u in range(5)
+                    ]
+                    cols = slice(cr * 128, cr * 128 + 128)
+                    for u in range(4):
+                        for par in range(2):
+                            y = jnp.where(odd16, tile[u], tile[u + 1]) if par else tile[u]
+                            hi, lo = halves(y * row[2 * u + par])
+                            to = (2 * u + n) * 16
+                            h_ref[par, rg, to : to + 16, cols] = hi
+                            h_ref[par, rg, 128 + to : 144 + to, cols] = lo
+
+    def multiply(units, h_ref):
         for rg in range(2):
-            acc = mm(h_ref[rg], wb[rg])
-            acc = acc[:384] + acc[384:]
-            rows[rg] = (acc[:, :128] + acc[:, 128:]).reshape(8, 48, 128)
-            for a in range(3):
+            for par in range(2):
+                acc = mm(h_ref[par, rg], wb[par, rg])
+                acc = acc[:128] + acc[128:]
+                acc = (acc[:, :128] + acc[:, 128:]).reshape(4, 32, 128)
+                for u in range(4):
+                    rows[rg, 2 * u + par] = acc[u]
+            for n, (t, a) in enumerate(units):
                 o = jnp.zeros((8, 128), F32)
                 for r16 in range(16):
-                    o = jnp.where(lane8 % 16 == r16, rows[rg, :, a * 16 + r16, :], o)
+                    o = jnp.where(lane8 % 16 == r16, rows[rg, :, n * 16 + r16, :], o)
                 octets[t, rg, a] = o
 
     def pass_on(t):
@@ -321,14 +326,44 @@
             device_id={"fer": octet(t)}, device_id_type=MESH,
         )
 
-    build(0, h0)
+    def first(t):
+        return [(2 * t, 0), (2 * t + 1, 0)]
+
+    def others(t):
+        return [(t, 1), (t, 2)]
+
+    mine_a.wait()
+    arrived(ra_in, 1)
+    for ac in range(3):
+        gt[ac] = ra_in[:, ac, :].T
+    v = ra_in[0:64, 3, :]
+    vert[0] = v
+    lane64 = lax.broadcasted_iota(jnp.int32, (64, 128), 1)
+    vert[1] = jnp.where(lane64 % 2 == 0, pltpu.roll(v, 127, axis=1), pltpu.roll(v, 1, axis=1))
+
+    build(first(0), h0)
+
+    def pair_first(t, carry):
+        build(first(2 * t + 1), h1)
+        multiply(first(2 * t), h0)
+        build(first(jnp.minimum(2 * t + 2, 3)), h0)
+        multiply(first(2 * t + 1), h1)
+        return carry
+
+    lax.fori_loop(0, 2, pair_first, 0)
+
+    mine_b.wait()
+    arrived(rb_in, 2)
+    for ac in range(3, 9):
+        gt[ac] = rb_in[:, ac - 3, :].T
+    build(others(0), h0)
 
     def pair(t, carry):
-        build(2 * t + 1, h1)
-        multiply(2 * t, h0)
+        build(others(2 * t + 1), h1)
+        multiply(others(2 * t), h0)
         pass_on(2 * t).start()
-        build(jnp.minimum(2 * t + 2, 7), h0)
-        multiply(2 * t + 1, h1)
+        build(others(jnp.minimum(2 * t + 2, 7)), h0)
+        multiply(others(2 * t + 1), h1)
 
         @pl.when(t < 3)
         def _():
@@ -407,19 +442,19 @@
             pltpu.VMEM((8, 128), F32),
             pltpu.VMEM((BOS, 8, 128), F32),
             pltpu.VMEM((8, 128), F32),
+            pltpu.VMEM((L, 2, 4, 128), F32),
+            pltpu.VMEM((L, 2, 6, 128), F32),
             pltpu.VMEM((L, 2, 5, 128), F32),
-            pltpu.VMEM((L, 2, 5, 128), F32),
-            pltpu.VMEM((L, 2, 5, 128), F32),
-            pltpu.VMEM((128, 5, 128), F32),
-            pltpu.VMEM((128, 5, 128), F32),
+            pltpu.VMEM((128, 4, 128), F32),
+            pltpu.VMEM((128, 6, 128), F32),
             pltpu.VMEM((128, 5, 128), F32),
             pltpu.VMEM((9, 128, 128), F32),
-            pltpu.VMEM((5, 128, 128), F32),
-            pltpu.VMEM((2, 768, 256), BF16),
-            pltpu.VMEM((64, 128), F32),
-            pltpu.VMEM((2, 768, 768), BF16),
-            pltpu.VMEM((2, 768, 768), BF16),
-            pltpu.VMEM((2, 8, 48, 128), F32),
+            pltpu.VMEM((2, 5, 128, 128), F32),
+            pltpu.VMEM((2, 2, 768, 256), BF16),
+            pltpu.VMEM((2, 64, 128), F32),
+            pltpu.VMEM((2, 2, 256, 768), BF16),
+            pltpu.VMEM((2, 2, 256, 768), BF16),
+            pltpu.VMEM((2, 8, 32, 128), F32),
             pltpu.VMEM((FER, 2, 3, 8, 128), F32),
             pltpu.VMEM((FER, 2, 3, 8, 128), F32),
             pltpu.VMEM((128, 512), BF16),

time: 49.2 us -> 48 us (0.976)
  Pallas kernels: 46.7 us -> 45.6 us
    pallas_call x1, Pallas kernels: 46.7 us -> 45.6 us  [body(): pl.pallas_call(whole_kernel, out_shape=jax.ShapeDtypeStruct((4, 9, 8, 128...]
where the time goes in v5:
time: 48 us; the launch traced here: 47.8 us
  Pallas kernels  45.6 us (95%)
  local copies, waits for them, and re-layouts  1.58 us (3%)
  between operations  0.66 us (1%)
    pallas_call x1, Pallas kernels, body(): pl.pallas_call(whole_kernel, out_shape=jax.ShapeDtypeStruct((4, 9, 8, 128...  45.6 us
    unnamed x1, local copies, waits for them, and re-layouts  1.58 us

profile of v5, /device:TPU:1, one launch (start us, length us, event | category | flops | bytes accessed | tf_op | source)
XLA Modules:
  0.0 47.8 jit_solution(12345138621504025510)
XLA Ops:
  0.7 45.6 %dual_self_energy.1 = f32[4,9,8,128]{3,2,1,0:T(8,128)} custom-call(s32[16]{0:T(128)} %bo.1, s32[1]{0:T(128)S(6)} %copy.13.ws, bf16[2,2,8,9,4,128]{5,4,3,2,1,0:T(4,128)(2,1)} %bitcast.5, bf16[8,576,128]{2,1,0:T(8,128)(2,1)} %bitcast.3, f32[8,8]{1,0:T(8,128)} %vertex.1, bf16[2,128,128]{2,1,0:T(8,128)(2,1)} %constant.12.clone.g1h, ...), custom_call_target="tpu_custom_call" | custom-call | tf_op jit(solution)/shard_map/dual_self_energy/pallas_call | solution.py:434
  46.2 1.6 %copy.14 = f32[4,8,9,128]{3,1,2,0:T(8,128)} copy(f32[4,8,9,128]{3,1,2,0:T(8,128)} %bitcast.4) | data formatting | bytes 294912

commit v6 on v5

--- a/solution.py
+++ b/solution.py
@@ -99,30 +99,38 @@
 )
 
 
-def ring(axis, size, start):
-    me = lax.axis_index(axis)
+def rows_ring(j, start):
     copies = []
-    for i in range(1, size):
-        to = lax.rem(me + i, size)
+    for i, (_, y, x, c) in enumerate(o for o in FAR_FIRST if o[0] == 0 and o[1] < 2):
+        to = (
+            lax.rem(j // 8 + y, 2) * 8
+            + lax.rem(lax.rem(j // 2, 4) + x, 4) * 2
+            + lax.rem(lax.rem(j, 2) + c, 2)
+        )
         copies.append(
-            pltpu.make_async_remote_copy(device_id={axis: to}, device_id_type=MESH, **start(to, i))
+            pltpu.make_async_remote_copy(device_id={"bos": to}, device_id_type=MESH, **start(to, i))
         )
     return copies
 
 
-def transform(x, m1, m2, s_ref, row):
+def transform(x, m1, m2, s_ref, row, more=None):
     z = nt(m1[0], x) + nt(m1[1], x)
     hi, lo = halves(jnp.concatenate([z[:L], z[L:]], axis=1))
     y = mm(hi, m2[0]) + mm(hi, m2[1]) + mm(lo, m2[0])
     for half in range(2):
-        s_ref[:, half, row, :] = y[:, half * 128 : half * 128 + 128]
+        part = y[:, half * 128 : half * 128 + 128]
+        s_ref[:, half, row, :] = part if more is None else part + more
+
+
+def vertex_lane(vi):
+    return 32 + 8 * vi if vi < 4 else 64 + 8 * vi
 
 
 def whole_kernel(
     bo, ws, green, weight, vertex, g1h, g2h, w1h, w2h, mxh, myh, out,
-    g1, g2, w1, w2, mx, my, planes, vsend, vgot, vsum, sa, sb, sw, ra_in, rb_in, rw_in,
+    g1, g2, w1, w2, mx, my, planes, wx, sa, sb, sw, ra_in, rb_in, rw_in,
     gt, wk, wb, vert, h0, h1, rows, octets, b_in, lh, ll, quads, e_in, yh, yl,
-    csem, green_s, green_r, vert_s, vert_r, pos_s, pos_r, own, oct_s, oct_r, quad_s, quad_r, seen,
+    csem, green_s, green_r, pos_s, pos_r, own, oct_s, oct_r, quad_s, quad_r, seen,
 ):
     f, j = lax.axis_index("fer"), lax.axis_index("bos")
     me = j * FER + f
@@ -138,23 +146,28 @@
     loads = [
         pltpu.make_async_copy(a, b, csem.at[i])
         for i, (a, b) in enumerate(
-            ((w1h, w1), (w2h, w2), (g1h, g1), (g2h, g2), (mxh, mx), (myh, my))
+            (
+                (w1h, w1), (w2h, w2), (g1h, g1), (g2h, g2), (mxh, mx), (myh, my), (weight.at[f], wx),
+            )
         )
     ]
-    for c in loads:
-        c.start()
-
+    for i in (6, 0, 1, 2, 3, 4, 5):
+        loads[i].start()
+
+    lane8 = lax.broadcasted_iota(jnp.int32, (8, 128), 1)
+    wide = jnp.concatenate([vertex[...], jnp.zeros((8, 120), F32)], axis=1)
+    values = jnp.zeros((1, 128), F32)
+    for vi in range(8):
+        at = vertex_lane(vi)
+        moved = pltpu.roll(jnp.broadcast_to(wide[vi : vi + 1], (8, 128)), at, axis=1)
+        values = jnp.where(lane8[:1] // 8 == at // 8, moved[:1], values)
+    loads[6].wait()
     loads[0].wait()
     loads[1].wait()
-    for k in range(5):
-        if k < 4:
-            x = weight[f, 128 * k : 128 * k + 128]
-        else:
-            x = jnp.concatenate([weight[f, 512:576], jnp.zeros((64, 128), BF16)], axis=0)
-        transform(x, w1, w2, sw, k)
-    lane8 = lax.broadcasted_iota(jnp.int32, (8, 128), 1)
-    spread = jnp.concatenate([vertex[...]] * BOS, axis=1)
-    vsend[...] = jnp.where(lane8 // 8 == bo[j], spread, 0.0)
+    for k in range(4):
+        transform(wx[128 * k : 128 * k + 128], w1, w2, sw, k)
+    x = jnp.concatenate([wx[512:576], jnp.zeros((64, 128), BF16)], axis=0)
+    transform(x, w1, w2, sw, 4, values)
 
     pl.semaphore_wait(barrier, BOS + FER - 2)
     for i in range(1, FER):
@@ -162,8 +175,8 @@
 
     parts = (pl.ds(0, 3), pl.ds(3, 6))
     near = [
-        ring(
-            "bos", BOS,
+        rows_ring(
+            j,
             lambda to, i, h=h: dict(
                 src_ref=green.at[:, to // 8, lax.rem(to, 8), parts[h]],
                 dst_ref=planes.at[:, parts[h], j],
@@ -172,17 +185,10 @@
         )
         for h in range(2)
     ]
-    near[0] += ring(
-        "bos", BOS,
-        lambda to, i: dict(
-            src_ref=vsend, dst_ref=vgot.at[j], send_sem=vert_s.at[i], recv_sem=vert_r.at[i]
-        ),
-    )
     for c in near[0] + near[1]:
         c.start()
     kept = pltpu.make_async_copy(green.at[:, j // 8, lax.rem(j, 8)], planes.at[:, :, j], own.at[0])
     kept.start()
-    vgot[j] = vsend[...]
 
     pl.semaphore_wait(seen, FER - 1)
 
@@ -224,13 +230,6 @@
 
     for c in near[0]:
         c.wait()
-    total = vgot[0]
-    for i in range(1, BOS):
-        total = total + vgot[i]
-    vsum[...] = total
-    sa[:, :, 3, :] = jnp.broadcast_to(
-        vsum[pl.ds(lax.rem(j, 8), 1), :].reshape(1, 1, 128), (L, 2, 128)
-    )
     for ac in range(3):
         transform(planes_of(ac), g1, g2, sa, ac)
     mine_a = everywhere(sa, ra_in, 1)
@@ -271,6 +270,18 @@
                     wb[par, rg, at, 0:128] = hi
                     wb[par, rg, at, 128:256] = lo
 
+    table = [jnp.zeros((8, 128), F32) for _ in range(8)]
+    for i in range(BOS):
+        x = rw_in[pl.ds((i // 8) * 64 + i % 8, 8, stride=8), 4, :]
+        for vi in range(8):
+            moved = pltpu.roll(x, lax.rem(8 * bo[i] - vertex_lane(vi) + 128, 128), axis=1)
+            table[vi] = jnp.where(lane8 // 8 == bo[i], moved, table[vi])
+    for vi in range(8):
+        vert[0, pl.ds(vi, 8, stride=8), :] = table[vi]
+    v = vert[0]
+    lane64 = lax.broadcasted_iota(jnp.int32, (64, 128), 1)
+    vert[1] = jnp.where(lane64 % 2 == 0, pltpu.roll(v, 127, axis=1), pltpu.roll(v, 1, axis=1))
+
     s = ws[0]
     lane16 = lax.broadcasted_iota(jnp.int32, (16, 128), 1)
     odd16 = lane16 % 2 == 1
@@ -336,10 +347,6 @@
     arrived(ra_in, 1)
     for ac in range(3):
         gt[ac] = ra_in[:, ac, :].T
-    v = ra_in[0:64, 3, :]
-    vert[0] = v
-    lane64 = lax.broadcasted_iota(jnp.int32, (64, 128), 1)
-    vert[1] = jnp.where(lane64 % 2 == 0, pltpu.roll(v, 127, axis=1), pltpu.roll(v, 1, axis=1))
 
     build(first(0), h0)
 
@@ -392,8 +399,8 @@
     for b in range(3):
         y = nt(mx[0, b], lh[...]) + nt(mx[0, b], ll[...]) + nt(mx[1, b], lh[...])
         quads[:, :, b * 128 : b * 128 + 128] = y.reshape(BOS, 8, 128)
-    last = ring(
-        "bos", BOS,
+    last = rows_ring(
+        j,
         lambda to, i: dict(
             src_ref=quads.at[to], dst_ref=e_in.at[j], send_sem=quad_s.at[i], recv_sem=quad_r.at[i]
         ),
@@ -434,18 +441,16 @@
     out = pl.pallas_call(
         whole_kernel,
         out_shape=jax.ShapeDtypeStruct((4, 9, 8, 128), F32),
-        in_specs=[sm, sm, vm, vm, vm] + [hbm] * 6,
+        in_specs=[sm, sm, hbm, hbm, vm] + [hbm] * 6,
         out_specs=vm,
         scratch_shapes=[pltpu.VMEM(m.shape, BF16) for m in mats]
         + [
             pltpu.VMEM((2, 9, BOS, 4, 128), BF16),
-            pltpu.VMEM((8, 128), F32),
-            pltpu.VMEM((BOS, 8, 128), F32),
-            pltpu.VMEM((8, 128), F32),
-            pltpu.VMEM((L, 2, 4, 128), F32),
+            pltpu.VMEM((576, 128), BF16),
+            pltpu.VMEM((L, 2, 3, 128), F32),
             pltpu.VMEM((L, 2, 6, 128), F32),
             pltpu.VMEM((L, 2, 5, 128), F32),
-            pltpu.VMEM((128, 4, 128), F32),
+            pltpu.VMEM((128, 3, 128), F32),
             pltpu.VMEM((128, 6, 128), F32),
             pltpu.VMEM((128, 5, 128), F32),
             pltpu.VMEM((9, 128, 128), F32),
@@ -463,7 +468,7 @@
             pltpu.VMEM((BOS, 8, 384), F32),
             pltpu.VMEM((72, 512), BF16),
             pltpu.VMEM((72, 512), BF16),
-            dma((6,)), dma((2, BOS)), dma((2, BOS)), dma((BOS,)), dma((BOS,)), dma((3,)), dma((3,)), dma((4,)),
+            dma((7,)), dma((2, BOS)), dma((2, BOS)), dma((3,)), dma((3,)), dma((4,)),
             dma((FER,)), dma((FER,)), dma((BOS,)), dma((BOS,)), pltpu.SemaphoreType.REGULAR,
         ],
         compiler_params=pltpu.CompilerParams(

time: 48 us -> 46 us (0.958)
  Pallas kernels: 45.6 us -> 43.5 us
    pallas_call x1, Pallas kernels: 45.6 us -> 43.5 us  [body(): pl.pallas_call(whole_kernel, out_shape=jax.ShapeDtypeStruct((4, 9, 8, 128...]
where the time goes in v6:
time: 46 us; the launch traced here: 45.8 us
  Pallas kernels  43.5 us (95%)
  local copies, waits for them, and re-layouts  1.58 us (3%)
  between operations  0.66 us (1%)
    pallas_call x1, Pallas kernels, body(): pl.pallas_call(whole_kernel, out_shape=jax.ShapeDtypeStruct((4, 9, 8, 128...  43.5 us
    unnamed x1, local copies, waits for them, and re-layouts  1.58 us

profile of v6, /device:TPU:1, one launch (start us, length us, event | category | flops | bytes accessed | tf_op | source)
XLA Modules:
  0.0 45.8 jit_solution(11862892891741292964)
XLA Ops:
  0.7 43.5 %dual_self_energy.1 = f32[4,9,8,128]{3,2,1,0:T(8,128)} custom-call(s32[16]{0:T(128)} %bo.1, s32[1]{0:T(128)S(6)} %copy.13.ws, bf16[2,2,8,9,4,128]{5,4,3,2,1,0:T(4,128)(2,1)} %bitcast.5, bf16[8,576,128]{2,1,0:T(8,128)(2,1)} %bitcast.3, f32[8,8]{1,0:T(8,128)} %vertex.1, bf16[2,128,128]{2,1,0:T(8,128)(2,1)} %constant.12.clone.g1h, ...), custom_call_target="tpu_custom_call" | custom-call | tf_op jit(solution)/shard_map/dual_self_energy/pallas_call | solution.py:441
  44.2 1.6 %copy.14 = f32[4,8,9,128]{3,1,2,0:T(8,128)} copy(f32[4,8,9,128]{3,1,2,0:T(8,128)} %bitcast.4) | data formatting | bytes 294912

commit v7 on v6

--- a/solution.py
+++ b/solution.py
@@ -99,18 +99,27 @@
 )
 
 
+def octet_of(f, t):
+    u = lax.rem(t, 4)
+    dz = jnp.where(u == 3, 0, jnp.where(u == 2, 3, 2 - u))
+    return lax.rem(f // 2 + dz, 4) * 2 + lax.rem(f + 1 + t // 4, 2)
+
+
+def rows_order(j):
+    return [
+        lax.rem(j // 8 + y, 2) * 8
+        + lax.rem(lax.rem(j // 2, 4) + x, 4) * 2
+        + lax.rem(lax.rem(j, 2) + c, 2)
+        for _, y, x, c in FAR_FIRST
+        if _ == 0 and y < 2
+    ]
+
+
 def rows_ring(j, start):
-    copies = []
-    for i, (_, y, x, c) in enumerate(o for o in FAR_FIRST if o[0] == 0 and o[1] < 2):
-        to = (
-            lax.rem(j // 8 + y, 2) * 8
-            + lax.rem(lax.rem(j // 2, 4) + x, 4) * 2
-            + lax.rem(lax.rem(j, 2) + c, 2)
-        )
-        copies.append(
-            pltpu.make_async_remote_copy(device_id={"bos": to}, device_id_type=MESH, **start(to, i))
-        )
-    return copies
+    return [
+        pltpu.make_async_remote_copy(device_id={"bos": to}, device_id_type=MESH, **start(to, i))
+        for i, to in enumerate(rows_order(j))
+    ]
 
 
 def transform(x, m1, m2, s_ref, row, more=None):
@@ -138,11 +147,10 @@
     count = FER * BOS
 
     barrier = pltpu.get_barrier_semaphore()
-    for axis, size, mine in (("bos", BOS, j), ("fer", FER, f)):
-        for i in range(1, size):
-            pl.semaphore_signal(
-                barrier, inc=1, device_id={axis: lax.rem(mine + i, size)}, device_id_type=MESH
-            )
+    for to in [octet_of(f, t) for t in range(FER - 1)]:
+        pl.semaphore_signal(barrier, inc=1, device_id={"fer": to}, device_id_type=MESH)
+    for to in rows_order(j):
+        pl.semaphore_signal(barrier, inc=1, device_id={"bos": to}, device_id_type=MESH)
     loads = [
         pltpu.make_async_copy(a, b, csem.at[i])
         for i, (a, b) in enumerate(
@@ -287,9 +295,7 @@
     odd16 = lane16 % 2 == 1
 
     def octet(t):
-        u = lax.rem(t, 4)
-        dz = jnp.where(u == 3, 0, jnp.where(u == 2, 3, 2 - u))
-        return lax.rem(f // 2 + dz, 4) * 2 + lax.rem(f + 1 + t // 4, 2)
+        return octet_of(f, t)
 
     def build(units, h_ref):
         for n, (t, a) in enumerate(units):
@@ -368,17 +374,17 @@
     def pair(t, carry):
         build(others(2 * t + 1), h1)
         multiply(others(2 * t), h0)
+        build(others(2 * t + 2), h0)
+        multiply(others(2 * t + 1), h1)
         pass_on(2 * t).start()
-        build(others(jnp.minimum(2 * t + 2, 7)), h0)
-        multiply(others(2 * t + 1), h1)
-
-        @pl.when(t < 3)
-        def _():
-            pass_on(2 * t + 1).start()
-
+        pass_on(2 * t + 1).start()
         return carry
 
-    lax.fori_loop(0, 4, pair, 0)
+    lax.fori_loop(0, 3, pair, 0)
+    build(others(7), h1)
+    multiply(others(6), h0)
+    pass_on(6).start()
+    multiply(others(7), h1)
     b_in[f] = octets[7]
     for t in range(7):
         pass_on(t).wait()

time: 46 us -> 45.6 us (level)
  no operation moved by 1% of the time
where the time goes in v7:
time: 45.6 us; the launch traced here: 45.4 us
  Pallas kernels  43.1 us (95%)
  local copies, waits for them, and re-layouts  1.58 us (3%)
  between operations  0.66 us (1%)
    pallas_call x1, Pallas kernels, body(): pl.pallas_call(whole_kernel, out_shape=jax.ShapeDtypeStruct((4, 9, 8, 128...  43.1 us
    unnamed x1, local copies, waits for them, and re-layouts  1.58 us

profile of v7, /device:TPU:1, one launch (start us, length us, event | category | flops | bytes accessed | tf_op | source)
XLA Modules:
  0.0 45.4 jit_solution(7769674471380994366)
XLA Ops:
  0.7 43.1 %dual_self_energy.1 = f32[4,9,8,128]{3,2,1,0:T(8,128)} custom-call(s32[16]{0:T(128)} %bo.1, s32[1]{0:T(128)S(6)} %copy.13.ws, bf16[2,2,8,9,4,128]{5,4,3,2,1,0:T(4,128)(2,1)} %bitcast.5, bf16[8,576,128]{2,1,0:T(8,128)(2,1)} %bitcast.3, f32[8,8]{1,0:T(8,128)} %vertex.1, bf16[2,128,128]{2,1,0:T(8,128)(2,1)} %constant.12.clone.g1h, ...), custom_call_target="tpu_custom_call" | custom-call | tf_op jit(solution)/shard_map/dual_self_energy/pallas_call | solution.py:447
  43.8 1.6 %copy.14 = f32[4,8,9,128]{3,1,2,0:T(8,128)} copy(f32[4,8,9,128]{3,1,2,0:T(8,128)} %bitcast.4) | data formatting | bytes 294912

commit v8 on v7

--- a/solution.py
+++ b/solution.py
@@ -136,10 +136,10 @@
 
 
 def whole_kernel(
-    bo, ws, green, weight, vertex, g1h, g2h, w1h, w2h, mxh, myh, out,
+    boh, wsh, green, weight, vertex, g1h, g2h, w1h, w2h, mxh, myh, out,
     g1, g2, w1, w2, mx, my, planes, wx, sa, sb, sw, ra_in, rb_in, rw_in,
     gt, wk, wb, vert, h0, h1, rows, octets, b_in, lh, ll, quads, e_in, yh, yl,
-    csem, green_s, green_r, pos_s, pos_r, own, oct_s, oct_r, quad_s, quad_r, seen,
+    csem, green_s, green_r, pos_s, pos_r, own, oct_s, oct_r, quad_s, quad_r, seen, bo, ws,
 ):
     f, j = lax.axis_index("fer"), lax.axis_index("bos")
     me = j * FER + f
@@ -155,11 +155,11 @@
         pltpu.make_async_copy(a, b, csem.at[i])
         for i, (a, b) in enumerate(
             (
-                (w1h, w1), (w2h, w2), (g1h, g1), (g2h, g2), (mxh, mx), (myh, my), (weight.at[f], wx),
+                (w1h, w1), (w2h, w2), (g1h, g1), (g2h, g2), (mxh, mx), (myh, my), (weight.at[f], wx), (boh, bo), (wsh, ws),
             )
         )
     ]
-    for i in (6, 0, 1, 2, 3, 4, 5):
+    for i in (6, 0, 1, 2, 3, 4, 5, 7, 8):
         loads[i].start()
 
     lane8 = lax.broadcasted_iota(jnp.int32, (8, 128), 1)
@@ -178,9 +178,6 @@
     transform(x, w1, w2, sw, 4, values)
 
     pl.semaphore_wait(barrier, BOS + FER - 2)
-    for i in range(1, FER):
-        pl.semaphore_signal(seen, inc=1, device_id={"fer": lax.rem(f + i, FER)}, device_id_type=MESH)
-
     parts = (pl.ds(0, 3), pl.ds(3, 6))
     near = [
         rows_ring(
@@ -193,7 +190,11 @@
         )
         for h in range(2)
     ]
-    for c in near[0] + near[1]:
+    for c in near[0]:
+        c.start()
+    for i in range(1, FER):
+        pl.semaphore_signal(seen, inc=1, device_id={"fer": lax.rem(f + i, FER)}, device_id_type=MESH)
+    for c in near[1]:
         c.start()
     kept = pltpu.make_async_copy(green.at[:, j // 8, lax.rem(j, 8)], planes.at[:, :, j], own.at[0])
     kept.start()
@@ -247,6 +248,8 @@
         transform(planes_of(ac), g1, g2, sb, ac - 3)
     mine_b = everywhere(sb, rb_in, 2)
 
+    loads[7].wait()
+    loads[8].wait()
     mine_w.wait()
     arrived(rw_in, 0)
     lane = lax.broadcasted_iota(jnp.int32, (128, 128), 1)
@@ -441,13 +444,12 @@
         out_y_matrix(),
     ]
     vm = pl.BlockSpec(memory_space=pltpu.VMEM)
-    sm = pl.BlockSpec(memory_space=pltpu.SMEM)
     hbm = pl.BlockSpec(memory_space=pl.ANY)
     dma = pltpu.SemaphoreType.DMA
     out = pl.pallas_call(
         whole_kernel,
         out_shape=jax.ShapeDtypeStruct((4, 9, 8, 128), F32),
-        in_specs=[sm, sm, hbm, hbm, vm] + [hbm] * 6,
+        in_specs=[hbm, hbm, hbm, hbm, vm] + [hbm] * 6,
         out_specs=vm,
         scratch_shapes=[pltpu.VMEM(m.shape, BF16) for m in mats]
         + [
@@ -474,8 +476,9 @@
             pltpu.VMEM((BOS, 8, 384), F32),
             pltpu.VMEM((72, 512), BF16),
             pltpu.VMEM((72, 512), BF16),
-            dma((7,)), dma((2, BOS)), dma((2, BOS)), dma((3,)), dma((3,)), dma((4,)),
+            dma((9,)), dma((2, BOS)), dma((2, BOS)), dma((3,)), dma((3,)), dma((4,)),
             dma((FER,)), dma((FER,)), dma((BOS,)), dma((BOS,)), pltpu.SemaphoreType.REGULAR,
+            pltpu.SMEM((16,), jnp.int32), pltpu.SMEM((1,), jnp.int32),
         ],
         compiler_params=pltpu.CompilerParams(
             has_side_effects=True, collective_id=0, vmem_limit_bytes=VMEM_LIMIT

time: 45.6 us -> 45.4 us (level)
  no operation moved by 1% of the time
where the time goes in v8:
time: 45.4 us; the launch traced here: 45.3 us
  Pallas kernels  43 us (95%)
  local copies, waits for them, and re-layouts  1.58 us (3%)
  between operations  0.66 us (1%)
    pallas_call x1, Pallas kernels, body(): pl.pallas_call(whole_kernel, out_shape=jax.ShapeDtypeStruct((4, 9, 8, 128...  43 us
    unnamed x1, local copies, waits for them, and re-layouts  1.58 us

profile of v8, /device:TPU:1, one launch (start us, length us, event | category | flops | bytes accessed | tf_op | source)
XLA Modules:
  0.0 45.3 jit_solution(179325640941806785)
XLA Ops:
  0.7 43.0 %dual_self_energy.1 = f32[4,9,8,128]{3,2,1,0:T(8,128)} custom-call(s32[16]{0:T(128)} %boh.1, s32[1]{0:T(128)S(6)} %copy.13.wsh, bf16[2,2,8,9,4,128]{5,4,3,2,1,0:T(4,128)(2,1)} %bitcast.5, bf16[8,576,128]{2,1,0:T(8,128)(2,1)} %bitcast.3, f32[8,8]{1,0:T(8,128)} %vertex.1, bf16[2,128,128]{2,1,0:T(8,128)(2,1)} %constant.12.clone.g1h, ...), custom_call_target="tpu_custom_call" | custom-call | tf_op jit(solution)/shard_map/dual_self_energy/pallas_call | solution.py:449
  43.7 1.6 %copy.14 = f32[4,8,9,128]{3,1,2,0:T(8,128)} copy(f32[4,8,9,128]{3,1,2,0:T(8,128)} %bitcast.4) | data formatting | bytes 294912
